TPU v7x, 128 devices: a whole 4x4x4 slice. The times are simulated.
128 devices in a mesh: rep: 2 (over core), width: 8 (over y, x_lo), hid: 8 (over z, x_hi).
Axes of the slice: x: 4 (x_hi: 2, x_lo: 2; x = x_hi * 2 + x_lo), y: 4, z: 4, core: 2. Of those that a mesh axis runs over, the one named last changes fastest.
Arguments:
- tokens: float32 [256, 5120], P(('rep', 'hid'), 'width'), may hold values from -6 to 6
- cotangent: float32 [256, 5120], P(('rep', 'hid'), 'width'), may hold values from -6 to 6
- w_gate: float32 [5120, 6912], P('width', 'hid'), may hold values from -0.078125 to 0.078125
- w_up: float32 [5120, 6912], P('width', 'hid'), may hold values from -0.078125 to 0.078125
- w_down: float32 [6912, 5120], P('hid', 'width'), may hold values from -0.078125 to 0.078125
Outputs:
- output: float32 [256, 5120], P(('rep', 'hid'), 'width')
- grad_tokens: float32 [256, 5120], P(('rep', 'hid'), 'width')
- grad_gate: float32 [8, 2, 320, 6912], P('width', 'rep', None, 'hid')
- grad_up: float32 [8, 2, 320, 6912], P('width', 'rep', None, 'hid')
- grad_down: float32 [8, 2, 432, 5120], P('hid', 'rep', None, 'width')
All inputs are finite; a program needn't handle non-finite values.
Results may differ from a plain program's by a relative error of at most 0.00016.
Values sent between devices are 32-bit elements; how exact they have to be, the bound alone decides.
A program may use at most 64 MiB of HBM per device.

v0:
```python
import jax
import jax.numpy as jnp
from jax import lax
from jax.sharding import Mesh
from jax.sharding import PartitionSpec as P

HID = ("hid_0", "hid_1")
REP_HID = ("rep", "hid_0", "hid_1")


def in_one_piece(arrays, axis, dim, along):
    both = jnp.concatenate(arrays, axis=along)
    result, at, finished = (lax.all_gather(both, axis, axis=dim, tiled=True), 0, [])
    for a in arrays:
        finished.append(lax.slice_in_dim(result, at, at + a.shape[along], axis=along))
        at += a.shape[along]
    return tuple(finished)


def in_blocks(value, dim, devices):
    dims = value.shape
    tiles = value.reshape(*dims[:dim], devices, dims[dim] // devices, *dims[dim + 1 :])
    return jnp.moveaxis(tiles, dim, 0)


def sent_and_summed(value, axis, dim):
    tiles = in_blocks(value, dim, lax.axis_size(axis))
    arrived = lax.all_to_all(tiles, axis, split_axis=0, concat_axis=0, tiled=True)
    return arrived.sum(axis=0)


def in_one_piece_2(arrays, axis, dim, along):
    widths = [a.shape[along] for a in arrays]
    both = jnp.concatenate(arrays, axis=along)
    result = sent_and_summed(both, axis, dim)
    return tuple(jnp.split(result, [sum(widths[:k]) for k in range(1, len(widths))], axis=along))


def in_order(tiles, dim):
    dims = list(tiles.shape[1:])
    dims[dim] *= tiles.shape[0]
    return jnp.moveaxis(tiles, 0, dim).reshape(dims)


def sent_to_all(value, axis):
    devices = lax.axis_size(axis)
    return lax.all_to_all(
        jnp.broadcast_to(value[None], (devices, *value.shape)), axis, 0, 0, tiled=True
    )


def gathered_copies(value, axis, dim):
    return in_order(sent_to_all(value, axis), dim)


def sum_by_axis(running, axes):
    for axis in axes:
        running = lax.psum_scatter(running, axis, scatter_dimension=0, tiled=True)
    return running


def forward_dot(left, right):
    return jnp.dot(left, right, precision=lax.Precision.HIGHEST, preferred_element_type=jnp.float32)


def right_transposed(left, right):
    return lax.dot_general(
        left,
        right,
        (((1,), (1,)), ((), ())),
        precision=lax.Precision.HIGHEST,
        preferred_element_type=jnp.float32,
    )


def left_transposed(left, right):
    return lax.dot_general(
        left,
        right,
        (((0,), (0,)), ((), ())),
        precision=lax.Precision.HIGHEST,
        preferred_element_type=jnp.float32,
    )


def activate(gate, up):
    logistic = jax.nn.sigmoid(gate)
    return gate * logistic * up


def derivatives(gate, up, grad_hidden):
    logistic = jax.nn.sigmoid(gate)
    gate_grad = grad_hidden * up * logistic * (1.0 + gate * (1.0 - logistic))
    up_grad = grad_hidden * gate * logistic
    return (gate_grad, up_grad)


def shards(tokens, cotangent, w_gate, w_up, w_down):
    gathered_x, gathered_dy = in_one_piece((tokens, cotangent), HID, 0, 1)
    gate_part = forward_dot(gathered_x, w_gate)
    up_part = forward_dot(gathered_x, w_up)
    back_part = right_transposed(gathered_dy, w_down)
    gate_share, up_share, grad_share = in_one_piece_2(
        (gate_part, up_part, back_part), "width", 0, 1
    )
    hidden = gathered_copies(activate(gate_share, up_share), "width", 0)
    gate_piece, up_piece = derivatives(gate_share, up_share, grad_share)
    gate_grad, up_grad = in_one_piece((gate_piece, up_piece), "width", 0, 1)
    output = sum_by_axis(forward_dot(hidden, w_down), HID)
    grad_tokens = sent_and_summed(
        right_transposed(gate_grad, w_gate) + right_transposed(up_grad, w_up), HID, 0
    )
    half_width = w_gate.shape[0] // 2
    half_hidden = w_down.shape[0] // 2
    replica = lax.axis_index("rep")
    partner = 1 - replica
    x_send = lax.dynamic_slice_in_dim(gathered_x, partner * half_width, half_width, 1)
    hidden_send = lax.dynamic_slice_in_dim(hidden, partner * half_hidden, half_hidden, 1)
    x_pair, gate_pair, up_pair, hidden_pair, dy_pair = in_one_piece(
        (x_send, gate_grad, up_grad, hidden_send, gathered_dy), "rep", 0, 1
    )
    group_rows = gathered_x.shape[0]

    def partner_block(stacked):
        return lax.dynamic_slice_in_dim(stacked, partner * group_rows, group_rows, 0)

    x_own = lax.dynamic_slice_in_dim(gathered_x, replica * half_width, half_width, 1)
    hidden_own = lax.dynamic_slice_in_dim(hidden, replica * half_hidden, half_hidden, 1)
    x_far = partner_block(x_pair)
    grad_gate = left_transposed(x_own, gate_grad) + left_transposed(x_far, partner_block(gate_pair))
    grad_up = left_transposed(x_own, up_grad) + left_transposed(x_far, partner_block(up_pair))
    grad_down = left_transposed(hidden_own, gathered_dy) + left_transposed(
        partner_block(hidden_pair), partner_block(dy_pair)
    )
    grad_gate = grad_gate.reshape(1, 1, half_width, grad_gate.shape[1])
    grad_up = grad_up.reshape(1, 1, half_width, grad_up.shape[1])
    grad_down = grad_down.reshape(1, 1, half_hidden, grad_down.shape[1])
    return (output, grad_tokens, grad_gate, grad_up, grad_down)


def solution(mesh):
    finer = Mesh(
        mesh.devices.reshape(mesh.shape["rep"], mesh.shape["width"], 4, 2),
        ("rep", "width", "hid_0", "hid_1"),
    )
    return jax.shard_map(
        shards,
        mesh=finer,
        in_specs=(
            P(REP_HID, "width"),
            P(REP_HID, "width"),
            P("width", HID),
            P("width", HID),
            P(HID, "width"),
        ),
        out_specs=(
            P(REP_HID, "width"),
            P(REP_HID, "width"),
            P("width", "rep", None, HID),
            P("width", "rep", None, HID),
            P(HID, "rep", None, "width"),
        ),
        check_vma=False,
    )
```

profile of v0, /device:TPU:0, one launch (start us, length us, event | category | flops | bytes accessed | tf_op | source)
XLA Modules:
  0.0 172.2 jit_solution(16794999661514566372)
XLA Ops:
  9.0 37.5 %all_gather.9 = f32[128,1280]{1,0:T(8,128)S(1)} all-gather(f32[16,1280]{1,0:T(8,128)S(1)} %pad_maximum_fusion.2), channel_id=1, replica_groups=mesh['rep'=2,'width'=8,'hid_0'=4,'hid_1'=2] {'hid_0','hid_1'}, dimensions={0}, use_global_device_ids=true | all-gather | bytes 737280 | tf_op jit(solution)/shard_map/all_gather | solution.py:13
  46.5 1.9 %fusion.27 = f32[128,864]{0,1:T(8,128)S(1)} fusion(f32[864,640]{1,0:T(8,128)S(1)} %copy-done, f32[128,1280]{1,0:T(8,128)S(1)} %all_gather.9), kind=kOutput, calls=%fused_computation.40 | convolution fusion | flops 849346560 | bytes 2981888 | tf_op jit(solution)/shard_map/dot_general | solution.py:67
  48.4 1.9 %fusion.29 = f32[128,864]{0,1:T(8,128)S(1)} fusion(f32[640,864]{0,1:T(8,128)S(1)} %copy-done.2, f32[128,1280]{1,0:T(8,128)S(1)} %all_gather.9), kind=kOutput, calls=%fused_computation.42 | convolution fusion | flops 849346560 | bytes 2981888 | tf_op jit(solution)/shard_map/dot_general | solution.py:63
  50.4 1.9 %fusion.31 = f32[128,864]{0,1:T(8,128)S(1)} fusion(f32[640,864]{0,1:T(8,128)S(1)} %copy-done.4, f32[128,1280]{1,0:T(8,128)S(1)} %all_gather.9), kind=kOutput, calls=%fused_computation.44 | convolution fusion | flops 849346560 | bytes 2981888 | tf_op jit(solution)/shard_map/dot_general | solution.py:63
  53.5 2.8 %copy.10 = f32[128,2592]{1,0:T(8,128)} copy(f32[128,2592]{0,1:T(8,128)} %pad_maximum_fusion) | data formatting | bytes 2654208 | tf_op jit(solution)/shard_map/concatenate | solution.py:34
  56.3 19.8 %all_to_all.15 = f32[8,16,2592]{2,1,0:T(8,128)} all-to-all(f32[8,16,2592]{2,1,0:T(8,128)} %bitcast.16), channel_id=1, replica_groups=mesh['rep'=2,'width'=8,'hid_0'=4,'hid_1'=2] {'width'}, dimensions={0} | all-to-all | bytes 2654208 | tf_op jit(solution)/shard_map/all_to_all | solution.py:28
  76.1 1.4 reduce_sum.18
  79.1 3.5 %all-to-all-start.1 = ((f32[8,16,864]{2,1,0:T(8,128)}), f32[8,16,864]{2,1,0:T(8,128)S(1)}, u32[]{:S(2)}, u32[]{:S(2)}) async-start(f32[8,16,864]{2,1,0:T(8,128)} %broadcast_in_dim.2), calls=%async_computation.1 | async-start | bytes 917504 | tf_op jit(solution)/shard_map/all_to_all | solution.py:47
  84.9 5.9 %all-to-all-done.1 = f32[8,16,864]{2,1,0:T(8,128)S(1)} async-done(((f32[8,16,864]{2,1,0:T(8,128)}), f32[8,16,864]{2,1,0:T(8,128)S(1)}, u32[]{:S(2)}, u32[]{:S(2)}) %all-to-all-start.1) | async-done | bytes 442400 | tf_op jit(solution)/shard_map/all_to_all | solution.py:47
  90.8 2.3 %fusion.35 = f32[128,640]{1,0:T(8,128)} fusion(f32[128,864]{1,0:T(8,128)S(1)} %bitcast.17, f32[864,640]{1,0:T(8,128)S(1)} %copy-done), kind=kOutput, calls=%fused_computation.48 | convolution fusion | flops 849346560 | bytes 2981888 | tf_op jit(solution)/shard_map/dot_general | solution.py:63
  93.3 31.1 %all_gather.10 = f32[128,1728]{1,0:T(8,128)S(1)} all-gather(f32[16,1728]{1,0:T(8,128)S(1)} %pad_maximum_fusion.1), channel_id=1, replica_groups=mesh['rep'=2,'width'=8,'hid_0'=4,'hid_1'=2] {'width'}, dimensions={0}, use_global_device_ids=true | all-gather | bytes 995328 | tf_op jit(solution)/shard_map/all_gather | solution.py:13
  125.3 2.4 %concatenate.16 = f32[128,3120]{1,0:T(8,128)} concatenate(f32[128,320]{1,0:T(8,128)} %constant_dynamic-slice_fusion.1, f32[128,1728]{1,0:T(8,128)S(1)} %all_gather.10, f32[128,432]{1,0:T(8,128)} %constant_dynamic-slice_fusion, f32[128,640]{1,0:T(8,128)S(1)} %copy-done.13), dimensions={1} | concatenate | bytes 3194880 | tf_op jit(solution)/shard_map/concatenate | solution.py:12
  127.8 3.4 %fusion.10 = f32[128,640]{1,0:T(8,128)S(1)} fusion(f32[640,864]{0,1:T(8,128)} %param.7, f32[128,1728]{1,0:T(8,128)S(1)} %all_gather.10), kind=kOutput, calls=%fused_computation.15 | convolution fusion | flops 849346560 | bytes 2998272 | tf_op jit(solution)/shard_map/dot_general | solution.py:67
  131.2 2.3 %convolution_add_fusion.3 = f32[128,640]{1,0:T(8,128)} fusion(f32[128,640]{1,0:T(8,128)S(1)} %fusion.10, f32[640,864]{0,1:T(8,128)S(1)} %copy-done.3, f32[128,1728]{1,0:T(8,128)S(1)} %all_gather.10), kind=kOutput, calls=%fused_computation.7 | convolution fusion | flops 849428480 | bytes 3325952 | tf_op jit(solution)/shard_map/dot_general | solution.py:67
  133.5 5.9 %all-to-all-start.2 = ((f32[8,16,640]{2,1,0:T(8,128)}), f32[8,16,640]{2,1,0:T(8,128)}, u32[]{:S(2)}, u32[]{:S(2)}) async-start(f32[8,16,640]{2,1,0:T(8,128)} %bitcast.20), calls=%async_computation.4 | async-start | bytes 655360 | tf_op jit(solution)/shard_map/all_to_all | solution.py:28
  139.5 2.4 %fusion.5 = f32[320,864]{1,0:T(8,128)} fusion(f32[128,1728]{1,0:T(8,128)S(1)} %all_gather.10, f32[128,640]{1,0:T(8,128)S(1)} %copy-done.12, s32[]{:T(128)S(6)} %select_n.19), kind=kOutput, calls=%fused_computation.10 | convolution fusion | flops 424673280 | bytes 1761284 | tf_op jit(solution)/shard_map/dot_general | solution.py:77
  141.9 2.2 %fusion.8 = f32[320,864]{1,0:T(8,128)} fusion(f32[128,1728]{1,0:T(8,128)S(1)} %all_gather.10, f32[128,640]{1,0:T(8,128)S(1)} %copy-done.12, s32[]{:T(128)S(6)} %select_n.19), kind=kOutput, calls=%fused_computation.13 | convolution fusion | flops 424673280 | bytes 1761284 | tf_op jit(solution)/shard_map/dot_general | solution.py:77
  144.1 4.6 %all-to-all-done.2 = f32[8,16,640]{2,1,0:T(8,128)} async-done(((f32[8,16,640]{2,1,0:T(8,128)}), f32[8,16,640]{2,1,0:T(8,128)}, u32[]{:S(2)}, u32[]{:S(2)}) %all-to-all-start.2) | async-done | bytes 327712 | tf_op jit(solution)/shard_map/all_to_all | solution.py:28
  148.7 1.6 reduce_sum.19
  150.3 3.3 %fusion.14 = f32[432,640]{1,0:T(8,128)} fusion(f32[128,864]{1,0:T(8,128)} %bitcast.18, s32[]{:T(128)S(6)} %select_n.23, f32[128,1280]{1,0:T(8,128)} %copy-done.1), kind=kOutput, calls=%fused_computation.19 | convolution fusion | flops 424673280 | bytes 1695748 | tf_op jit(solution)/shard_map/dot_general | solution.py:77
  153.7 2.2 %fusion.33 = (f32[256,864]{1,0:T(8,128)S(1)}, f32[256,864]{1,0:T(8,128)S(1)}) fusion(f32[256,3120]{1,0:T(8,128)} %all-gather.2.cloned.1.call-done), kind=kLoop, calls=%fused_computation.46 | loop fusion | bytes 3538944 | tf_op jit(solution)/shard_map/slice | solution.py:15
  157.0 2.1 %fusion = f32[1,1,320,864]{3,2,1,0:T(8,128)} fusion(f32[320,864]{1,0:T(8,128)S(1)} %copy-done.6, f32[256,864]{1,0:T(8,128)S(1)} %get-tuple-element.5, s32[]{:T(128)S(6)} %select_n.22, f32[256,320]{1,0:T(8,128)S(1)} %slice.41), kind=kOutput, calls=%fused_computation.1 | convolution fusion | flops 424949760 | bytes 2909184 | tf_op jit(solution)/shard_map/dot_general | solution.py:77
  160.5 2.1 %fusion.2 = f32[1,1,432,640]{3,2,1,0:T(8,128)} fusion(f32[432,640]{1,0:T(8,128)S(1)} %copy-done.9, f32[256,640]{1,0:T(8,128)S(1)} %slice.45, s32[]{:T(128)S(6)} %select_n.22, f32[256,432]{1,0:T(8,128)S(1)} %slice-done), kind=kOutput, calls=%fused_computation.5 | convolution fusion | flops 424949760 | bytes 2802688 | tf_op jit(solution)/shard_map/dot_general | solution.py:77
  162.6 2.1 %fusion.1 = f32[1,1,320,864]{3,2,1,0:T(8,128)} fusion(f32[320,864]{1,0:T(8,128)S(1)} %copy-done.5, f32[256,864]{1,0:T(8,128)S(1)} %get-tuple-element.6, s32[]{:T(128)S(6)} %select_n.22, f32[256,320]{1,0:T(8,128)S(1)} %slice.41), kind=kOutput, calls=%fused_computation.3 | convolution fusion | flops 424949760 | bytes 2909184 | tf_op jit(solution)/shard_map/dot_general | solution.py:77
  (51 shorter events, 9.6 us)
Async XLA Ops:
  8.0 38.5 %copy-start = (f32[864,640]{1,0:T(8,128)S(1)}, f32[864,640]{1,0:T(8,128)}, u32[]{:S(2)}) copy-start(f32[864,640]{1,0:T(8,128)} %param.9) | copy-start | bytes 6635524
  46.5 36.1 %copy-start.1 = (f32[128,1280]{1,0:T(8,128)}, f32[128,1280]{1,0:T(8,128)S(1)}, u32[]{:S(2)}) copy-start(f32[128,1280]{1,0:T(8,128)S(1)} %all_gather.9) | copy-start | bytes 1966084
  46.5 1.9 %copy-start.2 = (f32[640,864]{0,1:T(8,128)S(1)}, f32[640,864]{0,1:T(8,128)}, u32[]{:S(2)}) copy-start(f32[640,864]{0,1:T(8,128)} %param.8) | copy-start | bytes 6635524
  48.4 2.0 %copy-start.4 = (f32[640,864]{0,1:T(8,128)S(1)}, f32[640,864]{0,1:T(8,128)}, u32[]{:S(2)}) copy-start(f32[640,864]{0,1:T(8,128)} %param.7) | copy-start | bytes 6635524
  79.1 11.8 %all-to-all-start.1 = ((f32[8,16,864]{2,1,0:T(8,128)}), f32[8,16,864]{2,1,0:T(8,128)S(1)}, u32[]{:S(2)}, u32[]{:S(2)}) async-start(f32[8,16,864]{2,1,0:T(8,128)} %broadcast_in_dim.2), calls=%async_computation.1 | async-start | bytes 917504 | tf_op jit(solution)/shard_map/all_to_all | solution.py:47
  82.6 71.0 %reduce-scatter.3.cloned.1.call-start = ((), (), s32[]{:S(2)}) async-start(), calls=%async_computation.5 | async-start | bytes 409600 | tf_op jit(solution)/shard_map/reduce_scatter | solution.py:58
  83.4 0.7 copy-start.11
  90.8 2.3 %copy-start.7 = (f32[8,16,864]{2,1,0:T(8,128)}, f32[8,16,864]{2,1,0:T(8,128)S(1)}, u32[]{:S(2)}) copy-start(f32[8,16,864]{2,1,0:T(8,128)S(1)} %all-to-all-done.1) | copy-start | bytes 1327108
  90.8 2.4 %copy-start.14 = (f32[16,864]{1,0:T(8,128)S(1)}, f32[16,864]{1,0:T(8,128)}, u32[]{:S(2)}) copy-start(f32[16,864]{1,0:T(8,128)} %get-tuple-element.11) | copy-start | bytes 165892
  93.2 32.2 %copy-start.13 = (f32[128,640]{1,0:T(8,128)S(1)}, f32[128,640]{1,0:T(8,128)}, u32[]{:S(2)}) copy-start(f32[128,640]{1,0:T(8,128)} %get-tuple-element.7) | copy-start | bytes 983044
  93.2 60.5 %all-gather.2.cloned.1.call-start = ((), (), s32[]{:S(2)}) async-start(), calls=%async_computation.7 | async-start | bytes 4915200 | tf_op jit(solution)/shard_map/all_gather | solution.py:13
  93.2 31.2 %copy-start.8 = (f32[8,16,864]{2,1,0:T(8,128)S(1)}, f32[8,16,864]{2,1,0:T(8,128)}, u32[]{:S(2)}) copy-start(f32[8,16,864]{2,1,0:T(8,128)} %copy-done.7) | copy-start | bytes 1327108
  127.8 3.4 %copy-start.3 = (f32[640,864]{0,1:T(8,128)S(1)}, f32[640,864]{0,1:T(8,128)}, u32[]{:S(2)}) copy-start(f32[640,864]{0,1:T(8,128)} %param.8) | copy-start | bytes 6635524
  131.2 8.3 %copy-start.12 = (f32[128,640]{1,0:T(8,128)S(1)}, f32[128,640]{1,0:T(8,128)}, u32[]{:S(2)}) copy-start(f32[128,640]{1,0:T(8,128)} %copy-done.11) | copy-start | bytes 983044
  133.5 15.2 %all-to-all-start.2 = ((f32[8,16,640]{2,1,0:T(8,128)}), f32[8,16,640]{2,1,0:T(8,128)}, u32[]{:S(2)}, u32[]{:S(2)}) async-start(f32[8,16,640]{2,1,0:T(8,128)} %bitcast.20), calls=%async_computation.4 | async-start | bytes 655360 | tf_op jit(solution)/shard_map/all_to_all | solution.py:28
  139.5 25.3 %reduce-scatter.5.cloned.1.call-start = ((), (), s32[]{:S(2)}) async-start(), calls=%async_computation.6 | async-start | bytes 122880 | tf_op jit(solution)/shard_map/reduce_scatter | solution.py:58
  153.6 3.4 %copy-start.6 = (f32[320,864]{1,0:T(8,128)S(1)}, f32[320,864]{1,0:T(8,128)}, u32[]{:S(2)}) copy-start(f32[320,864]{1,0:T(8,128)} %fusion.5) | copy-start | bytes 3317764
  155.8 3.3 %copy-start.10 = (f32[256,3120]{1,0:T(8,128)S(1)}, f32[256,3120]{1,0:T(8,128)}, u32[]{:S(2)}) copy-start(f32[256,3120]{1,0:T(8,128)} %all-gather.2.cloned.1.call-done) | copy-start | bytes 9584644
  159.2 1.2 copy-start.9
  159.2 1.4 slice-start
  160.5 2.1 %copy-start.5 = (f32[320,864]{1,0:T(8,128)S(1)}, f32[320,864]{1,0:T(8,128)}, u32[]{:S(2)}) copy-start(f32[320,864]{1,0:T(8,128)} %fusion.8) | copy-start | bytes 3317764
Sparse Core Ops, SparseCore 0:
  93.3 20.4 reduce-scatter.2
  153.7 10.2 reduce-scatter.4
Sparse Core Ops, SparseCore 1:
  127.8 14.4 all-gather.1
where the time goes:
time: 173 us; the launch traced here: 172 us
  blocking collectives  88.5 us (51%)
  matrix products  28 us (16%)
  between operations  15.7 us (9%)
  local copies, waits for them, and re-layouts  13.9 us (8%)
  waiting for transfers between devices  10.6 us (6%)
  starting transfers between devices  9.54 us (6%)
  other arithmetic  5.94 us (3%)
    all_gather x2, blocking collectives, in_one_piece(): lax.all_gather(both, axis, axis=dim, tiled=True)  68.6 us
    all_to_all x1, blocking collectives, sent_and_summed(): lax.all_to_all(tiles, axis, split_axis=0, concat_axis=0, tiled=True)  19.8 us
    dot_general x6, matrix products, left_transposed(): lax.dot_general(left, right, (((0,), (0,)), ((), ())), precision=lax.Prec...  14.2 us
    dot_general x3, matrix products, right_transposed(): lax.dot_general(left, right, (((1,), (1,)), ((), ())), precision=lax.Prec...  7.64 us
    dot_general x3, matrix products, forward_dot(): jnp.dot(left, right, precision=lax.Precision.HIGHEST, preferred_element_t...  6.18 us
    all_to_all x1, starting transfers between devices, sent_and_summed(): lax.all_to_all(tiles, axis, split_axis=0, concat_axis=0, tiled=True)  5.95 us
    all_to_all x1, waiting for transfers between devices, sent_to_all(): lax.all_to_all(jnp.broadcast_to(value[None], (devices, *value.shape)), ax...  5.93 us
    all_to_all x1, waiting for transfers between devices, sent_and_summed(): lax.all_to_all(tiles, axis, split_axis=0, concat_axis=0, tiled=True)  4.61 us
  transfers between devices with their start and end apart: 5, of which 2 were waited for; matrix products, arithmetic and copies ran while one was open for 17% of the time, Pallas kernels for 0%

commit v1 on v0

v1 whole, which is shorter than its diff:
```python
import functools

import jax
import jax.numpy as jnp
from jax import lax
from jax.experimental import pallas as pl
from jax.experimental.pallas import tpu as pltpu
from jax.sharding import PartitionSpec as P

MESH = pl.DeviceIdType.MESH
F32 = jnp.float32
BF16 = jnp.bfloat16
NN = (((1,), (0,)), ((), ()))
NT = (((1,), (1,)), ((), ()))
ROWS = 128
W = 640
H = 864
HP = 896
X_OFFS = [(a, b) for a in range(4) for b in range(2) if (a, b) != (0, 0)]


def split(v):
    hi = v.astype(BF16)
    return hi, (v - hi.astype(F32)).astype(BF16)


def dot(a, b, dims):
    return lax.dot_general(a, b, dims, preferred_element_type=F32)


def dot3(stack, b_hi, b_lo, dims):
    m = stack.shape[0] // 2
    both = dot(stack, b_hi, dims)
    return both[:m] + both[m:] + dot(stack[:m], b_lo, dims)


def kernel(
    tok_in, cot_in, wg_in, wu_in, wd_in,
    out_o, gtok_o, gg_o, gu_o, gd_o,
    xf, df, xs, ds_, wgf, wuf, wdf, wgh, wgl, wuh, wul, wdh, wdl,
    part, r1, r2, r3, r4, s1, s3, own, full,
    xt, xt_far, dy_far, ht, ht_far, far,
    xth, xtl, hth, htl, bh, bl, dh, dl,
    op, gp, rg, o_own, g_own, wgrad, dgrad,
    a_s, a_r, c_s, c_r, e_s, e_r, g_s, g_r, p_s, p_r, l_s,
):
    rep = lax.axis_index("rep")
    w = lax.axis_index("width")
    h = lax.axis_index("hid")
    y, xl = w // 2, w % 2
    z, xh = h // 2, h % 2

    def ydev(k):
        return (rep, ((y + k) % 4) * 2 + xl, h)

    xdev = (rep, y * 2 + (1 - xl), h)

    def hdev(off):
        return (rep, w, ((z + off[0]) % 4) * 2 + (xh + off[1]) % 2)

    pdev = (1 - rep, w, h)
    sent = []

    def send(src, dst, s, r, device):
        c = pltpu.make_async_remote_copy(
            src_ref=src, dst_ref=dst, send_sem=s, recv_sem=r,
            device_id=device, device_id_type=MESH,
        )
        c.start()
        sent.append(c)
        return c

    def local(src, dst, i):
        c = pltpu.make_async_copy(src, dst, l_s.at[i])
        c.start()
        return c

    hrow = pl.multiple_of(h * 16, 16)
    lx = local(tok_in, xf.at[pl.ds(hrow, 16)], 0)
    ly = local(cot_in, df.at[pl.ds(hrow, 16)], 1)
    lg = local(wg_in, wgf, 2)
    lu = local(wu_in, wuf, 3)
    ld = local(wd_in, wdf, 4)

    barrier = pltpu.get_barrier_semaphore()
    peers = [ydev(k) for k in (1, 2, 3)] + [xdev] + [hdev(o) for o in X_OFFS] + [pdev]
    for d in peers:
        pl.semaphore_signal(barrier, inc=1, device_id=d, device_id_type=MESH)
    pl.semaphore_wait(barrier, len(peers))

    ax = [send(tok_in, xf.at[pl.ds(hrow, 16)], a_s.at[k], a_r.at[k], hdev(o)) for k, o in enumerate(X_OFFS)]
    ad = [send(cot_in, df.at[pl.ds(hrow, 16)], a_s.at[7 + k], a_r.at[7 + k], hdev(o)) for k, o in enumerate(X_OFFS)]

    def halves(src, hi_ref, lo_ref, rows, cols):
        step = 32

        def body(i, _):
            at = pl.multiple_of(i * step, step)
            hi, lo = split(src[pl.ds(at, step), :])
            hi_ref[pl.ds(at, step), pl.ds(0, cols)] = hi
            lo_ref[pl.ds(at, step), pl.ds(0, cols)] = lo
            return 0

        lax.fori_loop(0, rows // step, body, 0)

    for ref in (wgh, wgl, wuh, wul):
        ref[:, pl.ds(768, 128)] = jnp.zeros((W, 128), BF16)
    for ref in (wdh, wdl):
        ref[pl.ds(H, HP - H), :] = jnp.zeros((HP - H, W), BF16)
    lg.wait()
    halves(wgf, wgh, wgl, W, H)
    lu.wait()
    halves(wuf, wuh, wul, W, H)

    def scatter(a):
        c = [
            send(
                part.at[a, pl.ds(pl.multiple_of(32 * (1 - xl), 32), 32)], r1.at[a],
                c_s.at[a, 0], c_r.at[a, 0], xdev,
            )
        ]
        for k in (1, 2, 3):
            row = pl.multiple_of(64 + 16 * ((y + k) % 4), 16)
            c.append(
                send(part.at[a, pl.ds(row, 16)], r3.at[a, k - 1], c_s.at[a, k], c_r.at[a, k], ydev(k))
            )
        return c

    lx.wait()
    for c in ax:
        c.wait_recv()
    hi, lo = split(xf[...])
    xs[pl.ds(0, ROWS), :] = hi
    xs[pl.ds(ROWS, ROWS), :] = lo
    part[0] = dot3(xs[...], wgh[...], wgl[...], NN)
    c0 = scatter(0)
    part[1] = dot3(xs[...], wuh[...], wul[...], NN)
    c1 = scatter(1)
    ld.wait()
    halves(wdf, wdh, wdl, H, W)
    ly.wait()
    for c in ad:
        c.wait_recv()
    hi, lo = split(df[...])
    ds_[pl.ds(0, ROWS), :] = hi
    ds_[pl.ds(ROWS, ROWS), :] = lo
    part[2] = dot3(ds_[...], wdh[...], wdl[...], NT)
    c2 = scatter(2)
    p_dy = send(df, dy_far, p_s.at[0], p_r.at[0], pdev)

    def second(a, first):
        first[0].wait_recv()
        s1[a] = part[a, pl.ds(pl.multiple_of(32 * xl, 32), 32), :] + r1[a]
        c = []
        for k in (1, 2, 3):
            row = pl.multiple_of(8 * ((y + k) % 4), 8)
            c.append(
                send(s1.at[a, pl.ds(row, 8)], r2.at[a, k - 1], c_s.at[a, 3 + k], c_r.at[a, 3 + k], ydev(k))
            )
        for d in first[1:]:
            d.wait_recv()
        s3[a] = part[a, pl.ds(pl.multiple_of(64 + 16 * y, 16), 16), :] + r3[a, 0] + r3[a, 1] + r3[a, 2]
        c.append(
            send(
                s3.at[a, pl.ds(pl.multiple_of(8 * (1 - xl), 8), 8)], r4.at[a],
                c_s.at[a, 7], c_r.at[a, 7], xdev,
            )
        )
        return c

    def summed(a, c):
        for d in c:
            d.wait_recv()
        top = s1[a, pl.ds(pl.multiple_of(8 * y, 8), 8), :] + r2[a, 0] + r2[a, 1] + r2[a, 2]
        low = s3[a, pl.ds(pl.multiple_of(8 * xl, 8), 8), :] + r4[a]
        return jnp.concatenate([top, low], axis=0)

    top_row = pl.multiple_of(8 * (4 * xl + y), 8)
    low_row = pl.multiple_of(64 + 8 * (2 * y + xl), 8)
    low_pair = pl.multiple_of(64 + 16 * y, 16)
    top_half = pl.multiple_of(32 * xl, 32)

    def gather(a, value):
        full[a, pl.ds(top_row, 8), :] = value[:8]
        full[a, pl.ds(low_row, 8), :] = value[8:]
        c = [
            send(full.at[a, pl.ds(low_row, 8)], full.at[a, pl.ds(low_row, 8)], e_s.at[a, 0], e_r.at[a, 0], xdev)
        ]
        for k in (1, 2, 3):
            c.append(
                send(full.at[a, pl.ds(top_row, 8)], full.at[a, pl.ds(top_row, 8)], e_s.at[a, k], e_r.at[a, k], ydev(k))
            )
        return c

    def gather_on(a, first):
        first[0].wait_recv()
        c = []
        for k in (1, 2, 3):
            c.append(
                send(
                    full.at[a, pl.ds(low_pair, 16)], full.at[a, pl.ds(low_pair, 16)],
                    e_s.at[a, 3 + k], e_r.at[a, 3 + k], ydev(k),
                )
            )
        for d in first[1:]:
            d.wait_recv()
        c.append(
            send(
                full.at[a, pl.ds(top_half, 32)], full.at[a, pl.ds(top_half, 32)],
                e_s.at[a, 7], e_r.at[a, 7], xdev,
            )
        )
        return c

    d0 = second(0, c0)
    d1 = second(1, c1)
    d2 = second(2, c2)
    for j in range(5):
        xt[pl.ds(128 * j, 128), :] = xf[:, pl.ds(128 * j, 128)].T
    half_x = pl.multiple_of(320 * rep, 64)
    far_x = pl.multiple_of(320 * (1 - rep), 64)
    p_x = send(xt.at[pl.ds(far_x, 320)], xt_far, p_s.at[1], p_r.at[1], pdev)

    gate = summed(0, d0)
    up = summed(1, d1)
    logistic = 1.0 / (1.0 + jnp.exp(-gate))
    e0 = gather(0, gate * logistic * up)
    back = summed(2, d2)
    e1 = gather(1, back * up * logistic * (1.0 + gate * (1.0 - logistic)))
    e2 = gather(2, back * gate * logistic)

    f0 = gather_on(0, e0)
    f1 = gather_on(1, e1)
    f2 = gather_on(2, e2)

    def reduce_rows(src, i):
        c = []
        for k, o in enumerate(X_OFFS):
            row = pl.multiple_of(16 * (((z + o[0]) % 4) * 2 + (xh + o[1]) % 2), 16)
            c.append(send(src.at[pl.ds(row, 16)], rg.at[i, k], g_s.at[i, k], g_r.at[i, k], hdev(o)))
        return c

    for d in f0:
        d.wait_recv()
    hid = full[0]
    hi, lo = split(hid)
    op[...] = dot3(jnp.concatenate([hi, lo], axis=0), wdh[...], wdl[...], NN)
    g0 = reduce_rows(op, 0)
    for j in range(7):
        ht[pl.ds(128 * j, 128), :] = full[0, :, pl.ds(128 * j, 128)].T
    half_h = pl.multiple_of(432 * rep, 16)
    far_h = pl.multiple_of(432 * (1 - rep), 16)
    p_h = send(ht.at[pl.ds(far_h, 432)], ht_far, p_s.at[2], p_r.at[2], pdev)

    for d in f1:
        d.wait_recv()
    p_g = send(full.at[1], far.at[0], p_s.at[3], p_r.at[3], pdev)
    hi, lo = split(full[1])
    bh[0, pl.ds(0, ROWS), :] = hi
    bl[0, pl.ds(0, ROWS), :] = lo
    acc = dot3(jnp.concatenate([hi, lo], axis=0), wgh[...], wgl[...], NT)
    for d in f2:
        d.wait_recv()
    p_u = send(full.at[2], far.at[1], p_s.at[4], p_r.at[4], pdev)
    hi, lo = split(full[2])
    bh[1, pl.ds(0, ROWS), :] = hi
    bl[1, pl.ds(0, ROWS), :] = lo
    gp[...] = acc + dot3(jnp.concatenate([hi, lo], axis=0), wuh[...], wul[...], NT)
    g1 = reduce_rows(gp, 1)

    p_x.wait_recv()
    for ref, at in ((xt.at[pl.ds(half_x, 320)], 0), (xt_far, 128)):
        hi, lo = split(ref[...])
        xth[pl.ds(0, 320), pl.ds(at, 128)] = hi
        xth[pl.ds(320, 320), pl.ds(at, 128)] = lo
    p_dy.wait_recv()
    dh[pl.ds(0, ROWS), :] = ds_[pl.ds(0, ROWS), :]
    dl[pl.ds(0, ROWS), :] = ds_[pl.ds(ROWS, ROWS), :]
    hi, lo = split(dy_far[...])
    dh[pl.ds(ROWS, ROWS), :] = hi
    dl[pl.ds(ROWS, ROWS), :] = lo
    p_h.wait_recv()
    for ref, at in ((ht.at[pl.ds(half_h, 432)], 0), (ht_far, 128)):
        hi, lo = split(ref[...])
        hth[pl.ds(0, 432), pl.ds(at, 128)] = hi
        hth[pl.ds(432, 432), pl.ds(at, 128)] = lo
    dgrad[...] = dot3(hth[...], dh[...], dl[...], NN)
    o2 = local(dgrad, gd_o, 5)
    outs = [o2]
    for i, (c, o) in enumerate(((p_g, gg_o), (p_u, gu_o))):
        c.wait_recv()
        hi, lo = split(far[i])
        bh[i, pl.ds(ROWS, ROWS), :] = hi
        bl[i, pl.ds(ROWS, ROWS), :] = lo
        wgrad[i] = dot3(xth[...], bh[i], bl[i], NN)[:, :H]
        outs.append(local(wgrad.at[i], o, 6 + i))

    for i, (c, src, dst, o) in enumerate(((g0, op, o_own, out_o), (g1, gp, g_own, gtok_o))):
        for d in c:
            d.wait_recv()
        total = src[pl.ds(hrow, 16), :]
        for k in range(7):
            total = total + rg[i, k]
        dst[...] = total
        outs.append(local(dst, o, 8 + i))
    for c in outs:
        c.wait()
    for c in sent:
        c.wait_send()


def shards(tokens, cotangent, w_gate, w_up, w_down):
    v = pltpu.VMEM
    dma = pltpu.SemaphoreType.DMA
    scratch = [
        v((ROWS, W), F32), v((ROWS, W), F32), v((2 * ROWS, W), BF16), v((2 * ROWS, W), BF16),
        v((W, H), F32), v((W, H), F32), v((H, W), F32),
        v((W, HP), BF16), v((W, HP), BF16), v((W, HP), BF16), v((W, HP), BF16),
        v((HP, W), BF16), v((HP, W), BF16),
        v((3, ROWS, HP), F32), v((3, 32, HP), F32), v((3, 3, 8, HP), F32), v((3, 3, 16, HP), F32),
        v((3, 8, HP), F32), v((3, 32, HP), F32), v((3, 16, HP), F32), v((8, 128), F32), v((3, ROWS, HP), F32),
        v((W, ROWS), F32), v((320, ROWS), F32), v((ROWS, W), F32), v((HP, ROWS), F32), v((432, ROWS), F32),
        v((2, ROWS, HP), F32),
        v((640, 256), BF16), v((8, 128), BF16), v((864, 256), BF16), v((8, 128), BF16),
        v((2, 256, HP), BF16), v((2, 256, HP), BF16), v((256, W), BF16), v((256, W), BF16),
        v((ROWS, W), F32), v((ROWS, W), F32), v((2, 7, 16, W), F32), v((16, W), F32), v((16, W), F32),
        v((2, 320, H), F32), v((432, W), F32),
        dma((14,)), dma((14,)), dma((3, 8)), dma((3, 8)), dma((3, 8)), dma((3, 8)),
        dma((2, 7)), dma((2, 7)), dma((5,)), dma((5,)), dma((10,)),
    ]
    any_ = pl.BlockSpec(memory_space=pl.ANY)
    out, gtok, gg, gu, gd = pl.pallas_call(
        kernel,
        out_shape=[
            jax.ShapeDtypeStruct((16, W), F32), jax.ShapeDtypeStruct((16, W), F32),
            jax.ShapeDtypeStruct((320, H), F32), jax.ShapeDtypeStruct((320, H), F32),
            jax.ShapeDtypeStruct((432, W), F32),
        ],
        in_specs=[any_] * 5,
        out_specs=[any_] * 5,
        scratch_shapes=scratch,
        compiler_params=pltpu.CompilerParams(
            collective_id=0, has_side_effects=True, vmem_limit_bytes=56 << 20
        ),
    )(tokens, cotangent, w_gate, w_up, w_down)
    return out, gtok, gg[None, None], gu[None, None], gd[None, None]


def solution(mesh):
    return jax.shard_map(
        shards,
        mesh=mesh,
        in_specs=(
            P(("rep", "hid"), "width"), P(("rep", "hid"), "width"),
            P("width", "hid"), P("width", "hid"), P("hid", "width"),
        ),
        out_specs=(
            P(("rep", "hid"), "width"), P(("rep", "hid"), "width"),
            P("width", "rep", None, "hid"), P("width", "rep", None, "hid"),
            P("hid", "rep", None, "width"),
        ),
        check_vma=False,
    )
```

time: 173 us -> 65.1 us (0.38)
  blocking collectives: 88.5 us -> 0 us
  Pallas kernels: 0 us -> 50.8 us
  matrix products: 28 us -> 0 us
  between operations: 15.7 us -> 0.65 us
  waiting for transfers between devices: 10.6 us -> 0 us
  starting transfers between devices: 9.54 us -> 0 us
  other arithmetic: 5.94 us -> 0 us
    all_gather x2 -> x0, blocking collectives: 68.6 us -> none  [in_one_piece(): lax.all_gather(both, axis, axis=dim, tiled=True)]
    pallas_call x0 -> x1, Pallas kernels: none -> 50.8 us  [shards(): pl.pallas_call(kernel, out_shape=[jax.ShapeDtypeStruct((16, W), F32), jax...]
    dot_general x12 -> x0, matrix products: 28 us -> none  [the longest x6 14.2 us: left_transposed(): lax.dot_general(left, right, (((0,), (0,)), ((), ())), precision=lax.Prec...]
    all_to_all x1 -> x0, blocking collectives: 19.8 us -> none  [sent_and_summed(): lax.all_to_all(tiles, axis, split_axis=0, concat_axis=0, tiled=True)]
    unnamed x30 -> x13, local copies, waits for them, and re-layouts: 1.79 us -> 13.2 us
    all_to_all x2 -> x0, waiting for transfers between devices: 10.5 us -> none  [the longest x1 5.93 us: sent_to_all(): lax.all_to_all(jnp.broadcast_to(value[None], (devices, *value.shape)), ax...]
    all_to_all x2 -> x0, starting transfers between devices: 9.42 us -> none  [the longest x1 5.95 us: sent_and_summed(): lax.all_to_all(tiles, axis, split_axis=0, concat_axis=0, tiled=True)]
    concatenate x2 -> x0, local copies, waits for them, and re-layouts: 5.25 us -> none  [the longest x1 2.84 us: in_one_piece_2(): both = jnp.concatenate(arrays, axis=along)]
  transfers between devices with their start and end apart: 5 -> 0, of which waited for: 2 -> 0; matrix products, arithmetic and copies ran while one was open for 17% -> 0% of each run, Pallas kernels for 0% -> 0%
where the time goes in v1:
time: 65.1 us; the launch traced here: 64.7 us
  Pallas kernels  50.8 us (78%)
  local copies, waits for them, and re-layouts  13.2 us (20%)
    pallas_call x1, Pallas kernels, shards(): pl.pallas_call(kernel, out_shape=[jax.ShapeDtypeStruct((16, W), F32), jax...  50.8 us
    unnamed x13, local copies, waits for them, and re-layouts  13.2 us

profile of v1, /device:TPU:0, one launch (start us, length us, event | category | flops | bytes accessed | tf_op | source)
XLA Modules:
  0.0 64.7 jit_solution(666308258115368049)
XLA Ops:
  0.6 0.0 copy-start
  0.6 3.3 %copy.10.wg_in = f32[640,864]{1,0:T(8,128)} copy(f32[640,864]{0,1:T(8,128)} %param.7) | data formatting | bytes 4423680 | tf_op args[2]
  3.9 0.0 copy-done
  3.9 2.1 %copy.11.wu_in = f32[640,864]{1,0:T(8,128)} copy(f32[640,864]{0,1:T(8,128)S(1)} %copy-done) | data formatting | bytes 4423680 | tf_op args[3]
  6.0 50.8 %shard_map.92 = (f32[16,640]{1,0:T(8,128)}, f32[16,640]{1,0:T(8,128)}, f32[320,864]{1,0:T(8,128)}, f32[320,864]{1,0:T(8,128)}, f32[432,640]{1,0:T(8,128)}) custom-call(f32[16,640]{1,0:T(8,128)} %tok_in.1, f32[16,640]{1,0:T(8,128)} %cot_in.1, f32[640,864]{1,0:T(8,128)} %copy.10.wg_in, f32[640,864]{1,0:T(8,128)} %copy.11.wu_in, f32[864,640]{1,0:T(8,128)} %wd_in.1), custom_call_target="tpu_custom_call" | custom-call | tf_op jit(solution)/shard_map/pallas_call | solution.py:332
  56.9 1.4 %copy.17 = f32[16,640]{1,0:T(8,128)} copy(f32[16,640]{1,0:T(8,128)} %get-tuple-element.20) | data formatting | bytes 81920
  58.3 1.4 %copy.18 = f32[16,640]{1,0:T(8,128)} copy(f32[16,640]{1,0:T(8,128)} %get-tuple-element.21) | data formatting | bytes 81920
  59.7 0.0 copy-start.1
  59.7 2.4 %copy.19 = f32[1,1,320,864]{3,2,1,0:T(8,128)} copy(f32[1,1,320,864]{3,2,1,0:T(8,128)} %bitcast.4) | data formatting | bytes 2211840
  62.1 0.0 copy-done.1
  62.1 0.0 copy-start.2
  62.1 1.0 %copy.20 = f32[1,1,320,864]{3,2,1,0:T(8,128)} copy(f32[1,1,320,864]{3,2,1,0:T(8,128)S(1)} %bitcast.3) | data formatting | bytes 2211840
  63.1 0.7 %copy-done.2 = f32[432,640]{1,0:T(8,128)S(1)} copy-done((f32[432,640]{1,0:T(8,128)S(1)}, f32[432,640]{1,0:T(8,128)}, u32[]{:S(2)}) %copy-start.2) | copy-done | bytes 1105944
  63.8 1.0 %copy.21 = f32[1,1,432,640]{3,2,1,0:T(8,128)} copy(f32[1,1,432,640]{3,2,1,0:T(8,128)S(1)} %bitcast.5) | data formatting | bytes 2211840
Async XLA Ops:
  0.6 3.3 %copy-start = (f32[640,864]{0,1:T(8,128)S(1)}, f32[640,864]{0,1:T(8,128)}, u32[]{:S(2)}) copy-start(f32[640,864]{0,1:T(8,128)} %param.8) | copy-start | bytes 6635524
  59.7 2.4 %copy-start.1 = (f32[320,864]{1,0:T(8,128)S(1)}, f32[320,864]{1,0:T(8,128)}, u32[]{:S(2)}) copy-start(f32[320,864]{1,0:T(8,128)} %get-tuple-element.13) | copy-start | bytes 3317764
  62.1 1.7 %copy-start.2 = (f32[432,640]{1,0:T(8,128)S(1)}, f32[432,640]{1,0:T(8,128)}, u32[]{:S(2)}) copy-start(f32[432,640]{1,0:T(8,128)} %get-tuple-element.14) | copy-start | bytes 3317764

commit v2 on v1

--- a/solution.py
+++ b/solution.py
@@ -38,10 +38,10 @@
     tok_in, cot_in, wg_in, wu_in, wd_in,
     out_o, gtok_o, gg_o, gu_o, gd_o,
     xf, df, xs, ds_, wgf, wuf, wdf, wgh, wgl, wuh, wul, wdh, wdl,
-    part, r1, r2, r3, r4, s1, s3, own, full,
+    part, r1, r2, r3, r4, s1, s3, full,
     xt, xt_far, dy_far, ht, ht_far, far,
-    xth, xtl, hth, htl, bh, bl, dh, dl,
-    op, gp, rg, o_own, g_own, wgrad, dgrad,
+    xth, hth, bh, bl, dh, dl,
+    op, gp, rg,
     a_s, a_r, c_s, c_r, e_s, e_r, g_s, g_r, p_s, p_r, l_s,
 ):
     rep = lax.axis_index("rep")
@@ -91,26 +91,24 @@
     ax = [send(tok_in, xf.at[pl.ds(hrow, 16)], a_s.at[k], a_r.at[k], hdev(o)) for k, o in enumerate(X_OFFS)]
     ad = [send(cot_in, df.at[pl.ds(hrow, 16)], a_s.at[7 + k], a_r.at[7 + k], hdev(o)) for k, o in enumerate(X_OFFS)]
 
-    def halves(src, hi_ref, lo_ref, rows, cols):
+    def halves(src, hi_ref, lo_ref):
         step = 32
 
         def body(i, _):
             at = pl.multiple_of(i * step, step)
             hi, lo = split(src[pl.ds(at, step), :])
-            hi_ref[pl.ds(at, step), pl.ds(0, cols)] = hi
-            lo_ref[pl.ds(at, step), pl.ds(0, cols)] = lo
+            hi_ref[pl.ds(at, step), :] = hi
+            lo_ref[pl.ds(at, step), :] = lo
             return 0
 
-        lax.fori_loop(0, rows // step, body, 0)
-
-    for ref in (wgh, wgl, wuh, wul):
-        ref[:, pl.ds(768, 128)] = jnp.zeros((W, 128), BF16)
-    for ref in (wdh, wdl):
+        lax.fori_loop(0, H // step, body, 0)
+
+    for ref in (wgh, wgl, wuh, wul, wdh, wdl):
         ref[pl.ds(H, HP - H), :] = jnp.zeros((HP - H, W), BF16)
     lg.wait()
-    halves(wgf, wgh, wgl, W, H)
+    halves(wgf, wgh, wgl)
     lu.wait()
-    halves(wuf, wuh, wul, W, H)
+    halves(wuf, wuh, wul)
 
     def scatter(a):
         c = [
@@ -132,12 +130,12 @@
     hi, lo = split(xf[...])
     xs[pl.ds(0, ROWS), :] = hi
     xs[pl.ds(ROWS, ROWS), :] = lo
-    part[0] = dot3(xs[...], wgh[...], wgl[...], NN)
+    part[0] = dot3(xs[...], wgh[...], wgl[...], NT)
     c0 = scatter(0)
-    part[1] = dot3(xs[...], wuh[...], wul[...], NN)
+    part[1] = dot3(xs[...], wuh[...], wul[...], NT)
     c1 = scatter(1)
     ld.wait()
-    halves(wdf, wdh, wdl, H, W)
+    halves(wdf, wdh, wdl)
     ly.wait()
     for c in ad:
         c.wait_recv()
@@ -258,14 +256,14 @@
     hi, lo = split(full[1])
     bh[0, pl.ds(0, ROWS), :] = hi
     bl[0, pl.ds(0, ROWS), :] = lo
-    acc = dot3(jnp.concatenate([hi, lo], axis=0), wgh[...], wgl[...], NT)
+    acc = dot3(jnp.concatenate([hi, lo], axis=0), wgh[...], wgl[...], NN)
     for d in f2:
         d.wait_recv()
     p_u = send(full.at[2], far.at[1], p_s.at[4], p_r.at[4], pdev)
     hi, lo = split(full[2])
     bh[1, pl.ds(0, ROWS), :] = hi
     bl[1, pl.ds(0, ROWS), :] = lo
-    gp[...] = acc + dot3(jnp.concatenate([hi, lo], axis=0), wuh[...], wul[...], NT)
+    gp[...] = acc + dot3(jnp.concatenate([hi, lo], axis=0), wuh[...], wul[...], NN)
     g1 = reduce_rows(gp, 1)
 
     p_x.wait_recv()
@@ -284,29 +282,31 @@
         hi, lo = split(ref[...])
         hth[pl.ds(0, 432), pl.ds(at, 128)] = hi
         hth[pl.ds(432, 432), pl.ds(at, 128)] = lo
-    dgrad[...] = dot3(hth[...], dh[...], dl[...], NN)
-    o2 = local(dgrad, gd_o, 5)
-    outs = [o2]
+    gd_o[...] = dot3(hth[...], dh[...], dl[...], NN)
     for i, (c, o) in enumerate(((p_g, gg_o), (p_u, gu_o))):
         c.wait_recv()
         hi, lo = split(far[i])
         bh[i, pl.ds(ROWS, ROWS), :] = hi
         bl[i, pl.ds(ROWS, ROWS), :] = lo
-        wgrad[i] = dot3(xth[...], bh[i], bl[i], NN)[:, :H]
-        outs.append(local(wgrad.at[i], o, 6 + i))
-
-    for i, (c, src, dst, o) in enumerate(((g0, op, o_own, out_o), (g1, gp, g_own, gtok_o))):
+        o[...] = dot3(xth[...], bh[i], bl[i], NN)[:, :H]
+
+    for i, (c, src, o) in enumerate(((g0, op, out_o), (g1, gp, gtok_o))):
         for d in c:
             d.wait_recv()
         total = src[pl.ds(hrow, 16), :]
         for k in range(7):
             total = total + rg[i, k]
-        dst[...] = total
-        outs.append(local(dst, o, 8 + i))
-    for c in outs:
-        c.wait()
+        o[...] = total
     for c in sent:
         c.wait_send()
+
+
+def write(*refs):
+    copies = [pltpu.make_async_copy(refs[i], refs[5 + i], refs[10].at[i]) for i in range(5)]
+    for c in copies:
+        c.start()
+    for c in copies:
+        c.wait()
 
 
 def shards(tokens, cotangent, w_gate, w_up, w_down):
@@ -314,35 +314,39 @@
     dma = pltpu.SemaphoreType.DMA
     scratch = [
         v((ROWS, W), F32), v((ROWS, W), F32), v((2 * ROWS, W), BF16), v((2 * ROWS, W), BF16),
-        v((W, H), F32), v((W, H), F32), v((H, W), F32),
-        v((W, HP), BF16), v((W, HP), BF16), v((W, HP), BF16), v((W, HP), BF16),
-        v((HP, W), BF16), v((HP, W), BF16),
+        *[v((H, W), F32)] * 3, *[v((HP, W), BF16)] * 6,
         v((3, ROWS, HP), F32), v((3, 32, HP), F32), v((3, 3, 8, HP), F32), v((3, 3, 16, HP), F32),
-        v((3, 8, HP), F32), v((3, 32, HP), F32), v((3, 16, HP), F32), v((8, 128), F32), v((3, ROWS, HP), F32),
+        v((3, 8, HP), F32), v((3, 32, HP), F32), v((3, 16, HP), F32), v((3, ROWS, HP), F32),
         v((W, ROWS), F32), v((320, ROWS), F32), v((ROWS, W), F32), v((HP, ROWS), F32), v((432, ROWS), F32),
         v((2, ROWS, HP), F32),
-        v((640, 256), BF16), v((8, 128), BF16), v((864, 256), BF16), v((8, 128), BF16),
+        v((640, 256), BF16), v((864, 256), BF16),
         v((2, 256, HP), BF16), v((2, 256, HP), BF16), v((256, W), BF16), v((256, W), BF16),
-        v((ROWS, W), F32), v((ROWS, W), F32), v((2, 7, 16, W), F32), v((16, W), F32), v((16, W), F32),
-        v((2, 320, H), F32), v((432, W), F32),
+        v((ROWS, W), F32), v((ROWS, W), F32), v((2, 7, 16, W), F32),
         dma((14,)), dma((14,)), dma((3, 8)), dma((3, 8)), dma((3, 8)), dma((3, 8)),
-        dma((2, 7)), dma((2, 7)), dma((5,)), dma((5,)), dma((10,)),
+        dma((2, 7)), dma((2, 7)), dma((5,)), dma((5,)), dma((5,)),
     ]
     any_ = pl.BlockSpec(memory_space=pl.ANY)
-    out, gtok, gg, gu, gd = pl.pallas_call(
+    vmem = pl.BlockSpec(memory_space=pltpu.VMEM)
+    hbm = pl.BlockSpec(memory_space=pltpu.HBM)
+    shapes = [(16, W), (16, W), (320, H), (320, H), (432, W)]
+    results = pl.pallas_call(
         kernel,
-        out_shape=[
-            jax.ShapeDtypeStruct((16, W), F32), jax.ShapeDtypeStruct((16, W), F32),
-            jax.ShapeDtypeStruct((320, H), F32), jax.ShapeDtypeStruct((320, H), F32),
-            jax.ShapeDtypeStruct((432, W), F32),
-        ],
-        in_specs=[any_] * 5,
-        out_specs=[any_] * 5,
+        out_shape=[v(s, F32) for s in shapes],
+        in_specs=[hbm] * 5,
+        out_specs=[vmem] * 5,
         scratch_shapes=scratch,
         compiler_params=pltpu.CompilerParams(
-            collective_id=0, has_side_effects=True, vmem_limit_bytes=56 << 20
+            collective_id=0, has_side_effects=True, vmem_limit_bytes=48 << 20
         ),
-    )(tokens, cotangent, w_gate, w_up, w_down)
+    )(*[pltpu.with_memory_space_constraint(a, pltpu.HBM) for a in (tokens, cotangent, w_gate.T, w_up.T, w_down)])
+    results = [pltpu.with_memory_space_constraint(r, pltpu.VMEM) for r in results]
+    out, gtok, gg, gu, gd = pl.pallas_call(
+        write,
+        out_shape=[jax.ShapeDtypeStruct(s, F32) for s in shapes],
+        in_specs=[vmem] * 5,
+        out_specs=[any_] * 5,
+        scratch_shapes=[dma((5,))],
+    )(*results)
     return out, gtok, gg[None, None], gu[None, None], gd[None, None]
 
 

time: 65.1 us -> 53 us (0.81)
  local copies, waits for them, and re-layouts: 13.2 us -> 0 us
  Pallas kernels: 50.8 us -> 52.2 us
    unnamed x13 -> x0, local copies, waits for them, and re-layouts: 13.2 us -> none
    pallas_call x1 -> x2, Pallas kernels: 50.8 us -> 52.2 us  [the longest x1 50.4 us: shards(): pl.pallas_call(kernel, out_shape=[v(s, F32) for s in shapes], in_specs=[h...]
where the time goes in v2:
time: 53 us; the launch traced here: 52.8 us
  Pallas kernels  52.2 us (98%)
  between operations  0.64 us (1%)
    pallas_call x1, Pallas kernels, shards(): pl.pallas_call(kernel, out_shape=[v(s, F32) for s in shapes], in_specs=[h...  50.4 us
    pallas_call x1, Pallas kernels, shards(): pl.pallas_call(write, out_shape=[jax.ShapeDtypeStruct(s, F32) for s in sh...  1.82 us

profile of v2, /device:TPU:0, one launch (start us, length us, event | category | flops | bytes accessed | tf_op | source)
XLA Modules:
  0.0 52.8 jit_solution(15187705654846839611)
XLA Ops:
  0.6 50.4 %shard_map.92 = (f32[16,640]{1,0:T(8,128)S(1)}, f32[16,640]{1,0:T(8,128)S(1)}, f32[320,864]{1,0:T(8,128)S(1)}, f32[320,864]{1,0:T(8,128)S(1)}, f32[432,640]{1,0:T(8,128)S(1)}) custom-call(f32[16,640]{1,0:T(8,128)} %tok_in.1, f32[16,640]{1,0:T(8,128)} %cot_in.1, f32[864,640]{1,0:T(8,128)} %bitcast.5, f32[864,640]{1,0:T(8,128)} %bitcast.6, f32[864,640]{1,0:T(8,128)} %wd_in.1), custom_call_target="tpu_custom_call" | custom-call | tf_op jit(solution)/shard_map/pallas_call | solution.py:332
  51.0 1.8 %shard_map.93 = (f32[16,640]{1,0:T(8,128)}, f32[16,640]{1,0:T(8,128)}, f32[320,864]{1,0:T(8,128)}, f32[320,864]{1,0:T(8,128)}, f32[432,640]{1,0:T(8,128)}) custom-call(f32[16,640]{1,0:T(8,128)S(1)} %get-tuple-element.15.refs_0_, f32[16,640]{1,0:T(8,128)S(1)} %get-tuple-element.16.refs_1_, f32[320,864]{1,0:T(8,128)S(1)} %get-tuple-element.17.refs_2_, ...), custom_call_target="tpu_custom_call" | custom-call | tf_op jit(solution)/shard_map/pallas_call | solution.py:343

commit v3 on v2

v3 whole, which is shorter than its diff:
```python
import functools

import jax
import jax.numpy as jnp
from jax import lax
from jax.experimental import pallas as pl
from jax.experimental.pallas import tpu as pltpu
from jax.sharding import PartitionSpec as P

MESH = pl.DeviceIdType.MESH
F32 = jnp.float32
BF16 = jnp.bfloat16
NN = (((1,), (0,)), ((), ()))
NT = (((1,), (1,)), ((), ()))
ROWS = 128
W = 640
H = 864
HP = 896
C = 64
CX = 384
LX, LY = pl.ds(0, CX), pl.ds(CX, HP - CX)
GROUPS = ((0, 2), (2, 1))
GROUPS_BACK = ((0, 1), (1, 2))
H_OFFS = [(a, b) for a in range(4) for b in range(2) if (a, b) != (0, 0)]


def split(v):
    hi = v.astype(BF16)
    return hi, (v - hi.astype(F32)).astype(BF16)


def dot(a, b, dims):
    return lax.dot_general(a, b, dims, preferred_element_type=F32)


def dot3(stack, b_hi, b_lo, dims):
    m = stack.shape[0] // 2
    both = dot(stack, b_hi, dims)
    return both[:m] + both[m:] + dot(stack[:m], b_lo, dims)


def kernel(
    tok_in, cot_in, wg_in, wu_in, wd_in,
    out_o, gtok_o, gg_o, gu_o, gd_o,
    xf, df, xs, ds_, wgf, wuf, wdf, wgh, wgl, wuh, wul, wdh, wdl,
    part, r1, r2, r3, r4, s1, s3, full,
    xt, xt_far, dy_far, ht, ht_far, far,
    xth, hth, bh, bl, dh, dl,
    op, rg,
    a_s, a_r, c_s, c_r, e_s, e_r, g_s, g_r, p_s, p_r, l_s,
):
    rep = lax.axis_index("rep")
    w = lax.axis_index("width")
    h = lax.axis_index("hid")
    y, xl = w // 2, w % 2
    z, xh = h // 2, h % 2

    def ydev(k):
        return (rep, ((y + k) % 4) * 2 + xl, h)

    xdev = (rep, y * 2 + (1 - xl), h)

    def hindex(off):
        return ((z + off[0]) % 4) * 2 + (xh + off[1]) % 2

    def hdev(off):
        return (rep, w, hindex(off))

    pdev = (1 - rep, w, h)
    sent = []

    def send(src, dst, s, r, device):
        c = pltpu.make_async_remote_copy(
            src_ref=src, dst_ref=dst, send_sem=s, recv_sem=r,
            device_id=device, device_id_type=MESH,
        )
        c.start()
        sent.append(c)
        return c

    def local(src, dst, i):
        c = pltpu.make_async_copy(src, dst, l_s.at[i])
        c.start()
        return c

    def row8(k):
        return pl.ds(pl.multiple_of(8 * k, 8), 8)

    def arrived(copies):
        for d in copies:
            d.wait_recv()

    def rows_of(c):
        return pl.ds(pl.multiple_of(C * c + 8 * h, 8), 8)

    lx = [local(tok_in.at[pl.ds(8 * c, 8)], xf.at[rows_of(c)], c) for c in range(2)]
    ly = [local(cot_in.at[pl.ds(8 * c, 8)], df.at[rows_of(c)], 2 + c) for c in range(2)]
    lg = local(wg_in, wgf, 4)
    lu = local(wu_in, wuf, 5)
    ld = local(wd_in, wdf, 6)

    barrier = pltpu.get_barrier_semaphore()
    peers = [ydev(k) for k in (1, 2, 3)] + [xdev] + [hdev(o) for o in H_OFFS] + [pdev]
    for d in peers:
        pl.semaphore_signal(barrier, inc=1, device_id=d, device_id_type=MESH)
    pl.semaphore_wait(barrier, len(peers))

    def spread(src, dst, c, i):
        return [
            send(src.at[pl.ds(8 * c, 8)], dst.at[rows_of(c)], a_s.at[i, k], a_r.at[i, k], hdev(o))
            for k, o in enumerate(H_OFFS)
        ]

    ax, ad = [], []
    for c in range(2):
        ax.append(spread(tok_in, xf, c, 2 * c))
        ad.append(spread(cot_in, df, c, 2 * c + 1))

    def halves(src, hi_ref, lo_ref):
        step = 32

        def body(i, _):
            at = pl.multiple_of(i * step, step)
            hi, lo = split(src[pl.ds(at, step), :])
            hi_ref[pl.ds(at, step), :] = hi
            lo_ref[pl.ds(at, step), :] = lo
            return 0

        lax.fori_loop(0, H // step, body, 0)

    def stacked(src, dst, c):
        hi, lo = split(src[pl.ds(C * c, C), :])
        dst[c, pl.ds(0, C), :] = hi
        dst[c, pl.ds(C, C), :] = lo

    def halved(v):
        return v.reshape(2, C // 2, v.shape[1])

    def scatter(c, g):
        lo, n = GROUPS[g]
        arrays = pl.ds(lo, n)
        out = [
            send(
                part.at[c, arrays, 1 - xl, :, LX], r1.at[c, arrays],
                c_s.at[c, g, 0], c_r.at[c, g, 0], xdev,
            )
        ]
        for k in (1, 2, 3):
            out.append(
                send(
                    part.at[c, arrays, :, row8((y + k) % 4), LY], r3.at[c, k - 1, arrays],
                    c_s.at[c, g, k], c_r.at[c, g, k], ydev(k),
                )
            )
        return out

    def scatter_on(c, g, first):
        lo, n = GROUPS[g]
        arrays = pl.ds(lo, n)
        arrived(first[:1])
        for a in range(lo, lo + n):
            s1[c, a] = part[c, a, xl, :, LX] + r1[c, a]
        out = []
        for k in (1, 2, 3):
            out.append(
                send(
                    s1.at[c, arrays, row8((y + k) % 4)], r2.at[c, k - 1, arrays],
                    c_s.at[c, g, 3 + k], c_r.at[c, g, 3 + k], ydev(k),
                )
            )
        arrived(first[1:])
        for a in range(lo, lo + n):
            s3[c, a] = part[c, a, :, row8(y), LY] + r3[c, 0, a] + r3[c, 1, a] + r3[c, 2, a]
        out.append(
            send(
                s3.at[c, arrays, 1 - xl], r4.at[c, arrays],
                c_s.at[c, g, 7], c_r.at[c, g, 7], xdev,
            )
        )
        return out

    def summed(c, a):
        left = s1[c, a, row8(y), :] + r2[c, 0, a] + r2[c, 1, a] + r2[c, 2, a]
        right = s3[c, a, xl] + r4[c, a]
        return jnp.concatenate([left, right], axis=1)

    def gather(c, g):
        lo, n = GROUPS_BACK[g]
        arrays = pl.ds(lo, n)
        mine = full.at[c, arrays, xl, row8(y), LY]
        out = [send(mine, mine, e_s.at[c, g, 0], e_r.at[c, g, 0], xdev)]
        mine = full.at[c, arrays, xl, row8(y), LX]
        for k in (1, 2, 3):
            out.append(send(mine, mine, e_s.at[c, g, k], e_r.at[c, g, k], ydev(k)))
        return out

    def gather_on(c, g, first):
        lo, n = GROUPS_BACK[g]
        arrays = pl.ds(lo, n)
        out = []
        arrived(first[:1])
        pair = full.at[c, arrays, :, row8(y), LY]
        for k in (1, 2, 3):
            out.append(send(pair, pair, e_s.at[c, g, 3 + k], e_r.at[c, g, 3 + k], ydev(k)))
        arrived(first[1:])
        half = full.at[c, arrays, xl, :, LX]
        out.append(send(half, half, e_s.at[c, g, 7], e_r.at[c, g, 7], xdev))
        return out

    def activate(c):
        gate = summed(c, 0)
        up = summed(c, 1)
        logistic = 1.0 / (1.0 + jnp.exp(-gate))
        full[c, 0, xl, row8(y), :] = gate * logistic * up
        return gather(c, 0), (gate, up, logistic)

    def derive(c, saved):
        gate, up, logistic = saved
        back = summed(c, 2)
        full[c, 1, xl, row8(y), :] = back * up * logistic * (1.0 + gate * (1.0 - logistic))
        full[c, 2, xl, row8(y), :] = back * gate * logistic
        return gather(c, 1)

    def whole(c, a):
        return full[c, a].reshape(C, HP)

    def reduce_rows(i, c):
        return [
            send(
                op.at[i, c, row8(hindex(o))], rg.at[i, c, k],
                g_s.at[i, c, k], g_r.at[i, c, k], hdev(o),
            )
            for k, o in enumerate(H_OFFS)
        ]

    def project(c):
        hi, lo = split(whole(c, 0))
        op[0, c] = dot3(jnp.concatenate([hi, lo], axis=0), wdh[...], wdl[...], NN)
        return reduce_rows(0, c)

    def pull_back(c):
        acc = None
        for i, (wh, wl) in enumerate(((wgh, wgl), (wuh, wul))):
            hi, lo = split(whole(c, 1 + i))
            bh[i, pl.ds(C * c, C), :] = hi
            bl[i, pl.ds(C * c, C), :] = lo
            term = dot3(jnp.concatenate([hi, lo], axis=0), wh[...], wl[...], NN)
            acc = term if acc is None else acc + term
        op[1, c] = acc
        return reduce_rows(1, c)

    def gate_up(c):
        lx[c].wait()
        arrived(ax[c])
        stacked(xf, xs, c)
        part[c, 0] = halved(dot3(xs[c], wgh[...], wgl[...], NT))
        part[c, 1] = halved(dot3(xs[c], wuh[...], wul[...], NT))
        return scatter(c, 0)

    def back_part(c):
        ly[c].wait()
        arrived(ad[c])
        stacked(df, ds_, c)
        part[c, 2] = halved(dot3(ds_[c], wdh[...], wdl[...], NT))
        return scatter(c, 1)

    for ref in (wgh, wgl, wuh, wul, wdh, wdl):
        ref[pl.ds(H, HP - H), :] = jnp.zeros((HP - H, W), BF16)
    lg.wait()
    halves(wgf, wgh, wgl)
    lu.wait()
    halves(wuf, wuh, wul)
    c00 = gate_up(0)
    ld.wait()
    halves(wdf, wdh, wdl)
    c01 = back_part(0)
    c10 = gate_up(1)
    d00 = scatter_on(0, 0, c00)
    c11 = back_part(1)
    d01 = scatter_on(0, 1, c01)
    p_dy = send(df, dy_far, p_s.at[0], p_r.at[0], pdev)
    arrived(d00)
    e00, saved0 = activate(0)
    d10 = scatter_on(1, 0, c10)
    arrived(d01)
    e01 = derive(0, saved0)
    f00 = gather_on(0, 0, e00)
    d11 = scatter_on(1, 1, c11)
    arrived(d10)
    e10, saved1 = activate(1)
    f01 = gather_on(0, 1, e01)
    arrived(d11)
    e11 = derive(1, saved1)
    for j in range(5):
        xt[pl.ds(128 * j, 128), :] = xf[:, pl.ds(128 * j, 128)].T
    half_x = pl.multiple_of(320 * rep, 64)
    far_x = pl.multiple_of(320 * (1 - rep), 64)
    p_x = send(xt.at[pl.ds(far_x, 320)], xt_far, p_s.at[1], p_r.at[1], pdev)
    f10 = gather_on(1, 0, e10)
    arrived(f00)
    g00 = project(0)
    f11 = gather_on(1, 1, e11)
    arrived(f01)
    g10 = pull_back(0)
    arrived(f10)
    g01 = project(1)
    for j in range(7):
        lanes = pl.ds(128 * j, 128)
        block = jnp.concatenate([full[0, 0, :, :, lanes].reshape(C, 128), full[1, 0, :, :, lanes].reshape(C, 128)], axis=0)
        ht[pl.ds(128 * j, 128), :] = block.T
    half_h = pl.multiple_of(432 * rep, 16)
    far_h = pl.multiple_of(432 * (1 - rep), 16)
    p_h = send(ht.at[pl.ds(far_h, 432)], ht_far, p_s.at[2], p_r.at[2], pdev)
    arrived(f11)
    p_gu = send(full.at[:, pl.ds(1, 2)], far, p_s.at[3], p_r.at[3], pdev)
    g11 = pull_back(1)

    p_x.wait_recv()
    for ref, at in ((xt.at[pl.ds(half_x, 320)], 0), (xt_far, ROWS)):
        hi, lo = split(ref[...])
        xth[pl.ds(0, 320), pl.ds(at, ROWS)] = hi
        xth[pl.ds(320, 320), pl.ds(at, ROWS)] = lo
    p_dy.wait_recv()
    for c in range(2):
        dh[pl.ds(C * c, C), :] = ds_[c, pl.ds(0, C), :]
        dl[pl.ds(C * c, C), :] = ds_[c, pl.ds(C, C), :]
    hi, lo = split(dy_far[...])
    dh[pl.ds(ROWS, ROWS), :] = hi
    dl[pl.ds(ROWS, ROWS), :] = lo
    p_h.wait_recv()
    for ref, at in ((ht.at[pl.ds(half_h, 432)], 0), (ht_far, ROWS)):
        hi, lo = split(ref[...])
        hth[pl.ds(0, 432), pl.ds(at, ROWS)] = hi
        hth[pl.ds(432, 432), pl.ds(at, ROWS)] = lo
    gd_o[...] = dot3(hth[...], dh[...], dl[...], NN)
    p_gu.wait_recv()
    for i, o in enumerate((gg_o, gu_o)):
        for c in range(2):
            hi, lo = split(far[c, i].reshape(C, HP))
            bh[i, pl.ds(ROWS + C * c, C), :] = hi
            bl[i, pl.ds(ROWS + C * c, C), :] = lo
        o[...] = dot3(xth[...], bh[i], bl[i], NN)[:, :H]

    for i, c, copies, o in ((0, 0, g00, out_o), (1, 0, g10, gtok_o), (0, 1, g01, out_o), (1, 1, g11, gtok_o)):
        arrived(copies)
        total = op[i, c, row8(h), :]
        for k in range(7):
            total = total + rg[i, c, k]
        o[pl.ds(8 * c, 8), :] = total
    for c in sent:
        c.wait_send()


def write(*refs):
    copies = [pltpu.make_async_copy(refs[i], refs[5 + i], refs[10].at[i]) for i in range(5)]
    for c in copies:
        c.start()
    for c in copies:
        c.wait()


def shards(tokens, cotangent, w_gate, w_up, w_down):
    v = pltpu.VMEM
    dma = pltpu.SemaphoreType.DMA
    cy = HP - CX
    scratch = [
        v((ROWS, W), F32), v((ROWS, W), F32), v((2, 2 * C, W), BF16), v((2, 2 * C, W), BF16),
        *[v((H, W), F32)] * 3, *[v((HP, W), BF16)] * 6,
        v((2, 3, 2, 32, HP), F32), v((2, 3, 32, CX), F32), v((2, 3, 3, 8, CX), F32),
        v((2, 3, 3, 2, 8, cy), F32), v((2, 3, 8, cy), F32), v((2, 3, 32, CX), F32),
        v((2, 3, 2, 8, cy), F32), v((2, 3, 2, 32, HP), F32),
        v((W, ROWS), F32), v((320, ROWS), F32), v((ROWS, W), F32), v((HP, ROWS), F32), v((432, ROWS), F32),
        v((2, 2, 2, 32, HP), F32),
        v((640, 256), BF16), v((864, 256), BF16),
        v((2, 256, HP), BF16), v((2, 256, HP), BF16), v((256, W), BF16), v((256, W), BF16),
        v((2, 2, C, W), F32), v((2, 2, 7, 8, W), F32),
        dma((4, 7)), dma((4, 7)), dma((2, 2, 8)), dma((2, 2, 8)), dma((2, 2, 8)), dma((2, 2, 8)),
        dma((2, 2, 7)), dma((2, 2, 7)), dma((4,)), dma((4,)), dma((7,)),
    ]
    any_ = pl.BlockSpec(memory_space=pl.ANY)
    vmem = pl.BlockSpec(memory_space=pltpu.VMEM)
    hbm = pl.BlockSpec(memory_space=pltpu.HBM)
    shapes = [(16, W), (16, W), (320, H), (320, H), (432, W)]
    results = pl.pallas_call(
        kernel,
        out_shape=[v(s, F32) for s in shapes],
        in_specs=[hbm] * 5,
        out_specs=[vmem] * 5,
        scratch_shapes=scratch,
        compiler_params=pltpu.CompilerParams(
            collective_id=0, has_side_effects=True, vmem_limit_bytes=48 << 20
        ),
    )(*[pltpu.with_memory_space_constraint(a, pltpu.HBM) for a in (tokens, cotangent, w_gate.T, w_up.T, w_down)])
    results = [pltpu.with_memory_space_constraint(r, pltpu.VMEM) for r in results]
    out, gtok, gg, gu, gd = pl.pallas_call(
        write,
        out_shape=[jax.ShapeDtypeStruct(s, F32) for s in shapes],
        in_specs=[vmem] * 5,
        out_specs=[any_] * 5,
        scratch_shapes=[dma((5,))],
    )(*results)
    return out, gtok, gg[None, None], gu[None, None], gd[None, None]


def solution(mesh):
    return jax.shard_map(
        shards,
        mesh=mesh,
        in_specs=(
            P(("rep", "hid"), "width"), P(("rep", "hid"), "width"),
            P("width", "hid"), P("width", "hid"), P("hid", "width"),
        ),
        out_specs=(
            P(("rep", "hid"), "width"), P(("rep", "hid"), "width"),
            P("width", "rep", None, "hid"), P("width", "rep", None, "hid"),
            P("hid", "rep", None, "width"),
        ),
        check_vma=False,
    )
```

time: 53 us -> 54.4 us (1.026)
  Pallas kernels: 52.2 us -> 53.6 us
    pallas_call x1, Pallas kernels: 50.4 us -> 51.8 us  [shards(): pl.pallas_call(kernel, out_shape=[v(s, F32) for s in shapes], in_specs=[h...]
where the time goes in v3:
time: 54.4 us; the launch traced here: 54.3 us
  Pallas kernels  53.6 us (99%)
  between operations  0.64 us (1%)
    pallas_call x1, Pallas kernels, shards(): pl.pallas_call(kernel, out_shape=[v(s, F32) for s in shapes], in_specs=[h...  51.8 us
    pallas_call x1, Pallas kernels, shards(): pl.pallas_call(write, out_shape=[jax.ShapeDtypeStruct(s, F32) for s in sh...  1.82 us

profile of v3, /device:TPU:0, one launch (start us, length us, event | category | flops | bytes accessed | tf_op | source)
XLA Modules:
  0.0 54.3 jit_solution(10597541543243191810)
XLA Ops:
  0.6 51.8 %shard_map.92 = (f32[16,640]{1,0:T(8,128)S(1)}, f32[16,640]{1,0:T(8,128)S(1)}, f32[320,864]{1,0:T(8,128)S(1)}, f32[320,864]{1,0:T(8,128)S(1)}, f32[432,640]{1,0:T(8,128)S(1)}) custom-call(f32[16,640]{1,0:T(8,128)} %tok_in.1, f32[16,640]{1,0:T(8,128)} %cot_in.1, f32[864,640]{1,0:T(8,128)} %bitcast.5, f32[864,640]{1,0:T(8,128)} %bitcast.6, f32[864,640]{1,0:T(8,128)} %wd_in.1), custom_call_target="tpu_custom_call" | custom-call | tf_op jit(solution)/shard_map/pallas_call | solution.py:384
  52.5 1.8 %shard_map.93 = (f32[16,640]{1,0:T(8,128)}, f32[16,640]{1,0:T(8,128)}, f32[320,864]{1,0:T(8,128)}, f32[320,864]{1,0:T(8,128)}, f32[432,640]{1,0:T(8,128)}) custom-call(f32[16,640]{1,0:T(8,128)S(1)} %get-tuple-element.15.refs_0_, f32[16,640]{1,0:T(8,128)S(1)} %get-tuple-element.16.refs_1_, f32[320,864]{1,0:T(8,128)S(1)} %get-tuple-element.17.refs_2_, ...), custom_call_target="tpu_custom_call" | custom-call | tf_op jit(solution)/shard_map/pallas_call | solution.py:395

commit v4 on v3

--- a/solution.py
+++ b/solution.py
@@ -17,11 +17,14 @@
 H = 864
 HP = 896
 C = 64
-CX = 384
-LX, LY = pl.ds(0, CX), pl.ds(CX, HP - CX)
+CX = 512
+EX = 384
+SX, SY = pl.ds(0, CX), pl.ds(CX, HP - CX)
+GX, GY = pl.ds(0, EX), pl.ds(EX, HP - EX)
 GROUPS = ((0, 2), (2, 1))
 GROUPS_BACK = ((0, 1), (1, 2))
-H_OFFS = [(a, b) for a in range(4) for b in range(2) if (a, b) != (0, 0)]
+PIECES = (1, 1, 1, 1, 1)
+ORDER = ("fx", "gu0", "fd", "bk0", "gu1", "bk1", "s00", "s01", "s10", "s11", "act0", "dy", "der0", "act1", "der1", "f00", "f10", "f11", "f01", "pr0", "xt", "pr1", "pb1", "r01", "pb0", "r11", "ht")
 
 
 def split(v):
@@ -46,7 +49,7 @@
     part, r1, r2, r3, r4, s1, s3, full,
     xt, xt_far, dy_far, ht, ht_far, far,
     xth, hth, bh, bl, dh, dl,
-    op, rg,
+    op, rz, sz, rx,
     a_s, a_r, c_s, c_r, e_s, e_r, g_s, g_r, p_s, p_r, l_s,
 ):
     rep = lax.axis_index("rep")
@@ -60,12 +63,10 @@
 
     xdev = (rep, y * 2 + (1 - xl), h)
 
-    def hindex(off):
-        return ((z + off[0]) % 4) * 2 + (xh + off[1]) % 2
-
-    def hdev(off):
-        return (rep, w, hindex(off))
-
+    def zdev(k):
+        return (rep, w, ((z + k) % 4) * 2 + xh)
+
+    hdev = (rep, w, z * 2 + (1 - xh))
     pdev = (1 - rep, w, h)
     sent = []
 
@@ -90,31 +91,33 @@
         for d in copies:
             d.wait_recv()
 
-    def rows_of(c):
-        return pl.ds(pl.multiple_of(C * c + 8 * h, 8), 8)
-
-    lx = [local(tok_in.at[pl.ds(8 * c, 8)], xf.at[rows_of(c)], c) for c in range(2)]
-    ly = [local(cot_in.at[pl.ds(8 * c, 8)], df.at[rows_of(c)], 2 + c) for c in range(2)]
+    def ring(c, k=0):
+        return pl.ds(pl.multiple_of(C * c + 16 * ((z + k) % 4), 16), 16)
+
+    lx = local(tok_in, xf.at[ring(0)], 0)
+    ly = local(cot_in, df.at[ring(0)], 1)
     lg = local(wg_in, wgf, 4)
     lu = local(wu_in, wuf, 5)
     ld = local(wd_in, wdf, 6)
 
     barrier = pltpu.get_barrier_semaphore()
-    peers = [ydev(k) for k in (1, 2, 3)] + [xdev] + [hdev(o) for o in H_OFFS] + [pdev]
+    peers = [ydev(k) for k in (2, 1, 3)] + [xdev] + [zdev(k) for k in (2, 1, 3)] + [hdev] + [pdev]
     for d in peers:
         pl.semaphore_signal(barrier, inc=1, device_id=d, device_id_type=MESH)
     pl.semaphore_wait(barrier, len(peers))
 
-    def spread(src, dst, c, i):
-        return [
-            send(src.at[pl.ds(8 * c, 8)], dst.at[rows_of(c)], a_s.at[i, k], a_r.at[i, k], hdev(o))
-            for k, o in enumerate(H_OFFS)
-        ]
-
-    ax, ad = [], []
-    for c in range(2):
-        ax.append(spread(tok_in, xf, c, 2 * c))
-        ad.append(spread(cot_in, df, c, 2 * c + 1))
+    def spread(src, dst, i):
+        out = [send(src, dst.at[ring(0)], a_s.at[i, k], a_r.at[i, k], zdev(k)) for k in (2, 1, 3)]
+        out.append(send(src, dst.at[ring(1)], a_s.at[i, 0], a_r.at[i, 0], hdev))
+        return out
+
+    def spread_on(dst, i, first):
+        arrived(first[3:])
+        block = dst.at[ring(1)]
+        return [send(block, block, a_s.at[i, 3 + k], a_r.at[i, 3 + k], zdev(k)) for k in (2, 1, 3)]
+
+    ax = spread(tok_in, xf, 0)
+    ad = spread(cot_in, df, 1)
 
     def halves(src, hi_ref, lo_ref):
         step = 32
@@ -141,14 +144,14 @@
         arrays = pl.ds(lo, n)
         out = [
             send(
-                part.at[c, arrays, 1 - xl, :, LX], r1.at[c, arrays],
+                part.at[c, arrays, 1 - xl, :, SX], r1.at[c, arrays],
                 c_s.at[c, g, 0], c_r.at[c, g, 0], xdev,
             )
         ]
-        for k in (1, 2, 3):
+        for k in (2, 1, 3):
             out.append(
                 send(
-                    part.at[c, arrays, :, row8((y + k) % 4), LY], r3.at[c, k - 1, arrays],
+                    part.at[c, arrays, :, row8((y + k) % 4), SY], r3.at[c, k - 1, arrays],
                     c_s.at[c, g, k], c_r.at[c, g, k], ydev(k),
                 )
             )
@@ -159,9 +162,9 @@
         arrays = pl.ds(lo, n)
         arrived(first[:1])
         for a in range(lo, lo + n):
-            s1[c, a] = part[c, a, xl, :, LX] + r1[c, a]
+            s1[c, a] = part[c, a, xl, :, SX] + r1[c, a]
         out = []
-        for k in (1, 2, 3):
+        for k in (2, 1, 3):
             out.append(
                 send(
                     s1.at[c, arrays, row8((y + k) % 4)], r2.at[c, k - 1, arrays],
@@ -170,7 +173,7 @@
             )
         arrived(first[1:])
         for a in range(lo, lo + n):
-            s3[c, a] = part[c, a, :, row8(y), LY] + r3[c, 0, a] + r3[c, 1, a] + r3[c, 2, a]
+            s3[c, a] = part[c, a, :, row8(y), SY] + r3[c, 0, a] + r3[c, 1, a] + r3[c, 2, a]
         out.append(
             send(
                 s3.at[c, arrays, 1 - xl], r4.at[c, arrays],
@@ -187,10 +190,10 @@
     def gather(c, g):
         lo, n = GROUPS_BACK[g]
         arrays = pl.ds(lo, n)
-        mine = full.at[c, arrays, xl, row8(y), LY]
+        mine = full.at[c, arrays, xl, row8(y), GY]
         out = [send(mine, mine, e_s.at[c, g, 0], e_r.at[c, g, 0], xdev)]
-        mine = full.at[c, arrays, xl, row8(y), LX]
-        for k in (1, 2, 3):
+        mine = full.at[c, arrays, xl, row8(y), GX]
+        for k in (2, 1, 3):
             out.append(send(mine, mine, e_s.at[c, g, k], e_r.at[c, g, k], ydev(k)))
         return out
 
@@ -199,11 +202,11 @@
         arrays = pl.ds(lo, n)
         out = []
         arrived(first[:1])
-        pair = full.at[c, arrays, :, row8(y), LY]
-        for k in (1, 2, 3):
+        pair = full.at[c, arrays, :, row8(y), GY]
+        for k in (2, 1, 3):
             out.append(send(pair, pair, e_s.at[c, g, 3 + k], e_r.at[c, g, 3 + k], ydev(k)))
         arrived(first[1:])
-        half = full.at[c, arrays, xl, :, LX]
+        half = full.at[c, arrays, xl, :, GX]
         out.append(send(half, half, e_s.at[c, g, 7], e_r.at[c, g, 7], xdev))
         return out
 
@@ -226,12 +229,17 @@
 
     def reduce_rows(i, c):
         return [
-            send(
-                op.at[i, c, row8(hindex(o))], rg.at[i, c, k],
-                g_s.at[i, c, k], g_r.at[i, c, k], hdev(o),
-            )
-            for k, o in enumerate(H_OFFS)
+            send(op.at[i, c, ring(0, k)], rz.at[i, c, k - 1], g_s.at[i, c, k], g_r.at[i, c, k], zdev(k))
+            for k in (2, 1, 3)
         ]
+
+    def ring_sum(i, c):
+        return op[i, c, ring(0), :] + rz[i, c, 0] + rz[i, c, 1] + rz[i, c, 2]
+
+    def reduce_on(i, first):
+        arrived(first)
+        sz[i] = ring_sum(i, 1)
+        return [send(sz.at[i], rx.at[i], g_s.at[i, 0, 0], g_r.at[i, 0, 0], hdev)]
 
     def project(c):
         hi, lo = split(whole(c, 0))
@@ -250,16 +258,14 @@
         return reduce_rows(1, c)
 
     def gate_up(c):
-        lx[c].wait()
-        arrived(ax[c])
+        arrived(kept.pop(("x", c)))
         stacked(xf, xs, c)
         part[c, 0] = halved(dot3(xs[c], wgh[...], wgl[...], NT))
         part[c, 1] = halved(dot3(xs[c], wuh[...], wul[...], NT))
         return scatter(c, 0)
 
     def back_part(c):
-        ly[c].wait()
-        arrived(ad[c])
+        arrived(kept.pop(("d", c)))
         stacked(df, ds_, c)
         part[c, 2] = halved(dot3(ds_[c], wdh[...], wdl[...], NT))
         return scatter(c, 1)
@@ -270,70 +276,92 @@
     halves(wgf, wgh, wgl)
     lu.wait()
     halves(wuf, wuh, wul)
-    c00 = gate_up(0)
     ld.wait()
     halves(wdf, wdh, wdl)
-    c01 = back_part(0)
-    c10 = gate_up(1)
-    d00 = scatter_on(0, 0, c00)
-    c11 = back_part(1)
-    d01 = scatter_on(0, 1, c01)
-    p_dy = send(df, dy_far, p_s.at[0], p_r.at[0], pdev)
-    arrived(d00)
-    e00, saved0 = activate(0)
-    d10 = scatter_on(1, 0, c10)
-    arrived(d01)
-    e01 = derive(0, saved0)
-    f00 = gather_on(0, 0, e00)
-    d11 = scatter_on(1, 1, c11)
-    arrived(d10)
-    e10, saved1 = activate(1)
-    f01 = gather_on(0, 1, e01)
-    arrived(d11)
-    e11 = derive(1, saved1)
-    for j in range(5):
-        xt[pl.ds(128 * j, 128), :] = xf[:, pl.ds(128 * j, 128)].T
+    lx.wait()
+    ly.wait()
+    kept = {("x", 0): ax[:3], ("d", 0): ad[:3]}
+
+    def keep(name, value):
+        kept[name] = value
+
     half_x = pl.multiple_of(320 * rep, 64)
     far_x = pl.multiple_of(320 * (1 - rep), 64)
-    p_x = send(xt.at[pl.ds(far_x, 320)], xt_far, p_s.at[1], p_r.at[1], pdev)
-    f10 = gather_on(1, 0, e10)
-    arrived(f00)
-    g00 = project(0)
-    f11 = gather_on(1, 1, e11)
-    arrived(f01)
-    g10 = pull_back(0)
-    arrived(f10)
-    g01 = project(1)
-    for j in range(7):
-        lanes = pl.ds(128 * j, 128)
-        block = jnp.concatenate([full[0, 0, :, :, lanes].reshape(C, 128), full[1, 0, :, :, lanes].reshape(C, 128)], axis=0)
-        ht[pl.ds(128 * j, 128), :] = block.T
     half_h = pl.multiple_of(432 * rep, 16)
     far_h = pl.multiple_of(432 * (1 - rep), 16)
-    p_h = send(ht.at[pl.ds(far_h, 432)], ht_far, p_s.at[2], p_r.at[2], pdev)
-    arrived(f11)
-    p_gu = send(full.at[:, pl.ds(1, 2)], far, p_s.at[3], p_r.at[3], pdev)
-    g11 = pull_back(1)
-
-    p_x.wait_recv()
+
+    def do_activate(c):
+        arrived(kept.pop(("d", c, 0)))
+        copies, saved = activate(c)
+        keep(("e", c, 0), copies)
+        keep(("saved", c), saved)
+
+    def do_derive(c):
+        arrived(kept.pop(("d", c, 1)))
+        keep(("e", c, 1), derive(c, kept.pop(("saved", c))))
+
+    def do_project(c):
+        arrived(kept.pop(("f", c, 0)))
+        keep(("g", 0, c), project(c))
+
+    def do_pull_back(c):
+        arrived(kept.pop(("f", c, 1)))
+        keep(("pg", c), send(full.at[c, pl.ds(1, 2)], far.at[c], p_s.at[3 + c], p_r.at[3 + c], pdev))
+        keep(("g", 1, c), pull_back(c))
+
+    def turn_tokens():
+        for j in range(5):
+            xt[pl.ds(128 * j, 128), :] = xf[:, pl.ds(128 * j, 128)].T
+        keep("px", send(xt.at[pl.ds(far_x, 320)], xt_far, p_s.at[1], p_r.at[1], pdev))
+
+    def turn_hidden():
+        for j in range(7):
+            lanes = pl.ds(128 * j, 128)
+            block = [full[c, 0, :, :, lanes].reshape(C, 128) for c in range(2)]
+            ht[pl.ds(128 * j, 128), :] = jnp.concatenate(block, axis=0).T
+        keep("ph", send(ht.at[pl.ds(far_h, 432)], ht_far, p_s.at[2], p_r.at[2], pdev))
+
+    steps = {
+        "fx": lambda: keep(("x", 1), spread_on(xf, 0, ax)),
+        "fd": lambda: keep(("d", 1), spread_on(df, 1, ad)),
+        "dy": lambda: keep("py", send(df, dy_far, p_s.at[0], p_r.at[0], pdev)),
+        "xt": turn_tokens,
+        "ht": turn_hidden,
+        "r01": lambda: keep(("g", 0), reduce_on(0, kept.pop(("g", 0, 1)))),
+        "r11": lambda: keep(("g", 1), reduce_on(1, kept.pop(("g", 1, 1)))),
+    }
+    for c in range(2):
+        steps[f"gu{c}"] = lambda c=c: keep(("c", c, 0), gate_up(c))
+        steps[f"bk{c}"] = lambda c=c: keep(("c", c, 1), back_part(c))
+        steps[f"act{c}"] = lambda c=c: do_activate(c)
+        steps[f"der{c}"] = lambda c=c: do_derive(c)
+        steps[f"pr{c}"] = lambda c=c: do_project(c)
+        steps[f"pb{c}"] = lambda c=c: do_pull_back(c)
+        for g in range(2):
+            steps[f"s{c}{g}"] = lambda c=c, g=g: keep(("d", c, g), scatter_on(c, g, kept.pop(("c", c, g))))
+            steps[f"f{c}{g}"] = lambda c=c, g=g: keep(("f", c, g), gather_on(c, g, kept.pop(("e", c, g))))
+    for name in ORDER:
+        steps[name]()
+
+    kept["px"].wait_recv()
     for ref, at in ((xt.at[pl.ds(half_x, 320)], 0), (xt_far, ROWS)):
         hi, lo = split(ref[...])
         xth[pl.ds(0, 320), pl.ds(at, ROWS)] = hi
         xth[pl.ds(320, 320), pl.ds(at, ROWS)] = lo
-    p_dy.wait_recv()
+    kept["py"].wait_recv()
     for c in range(2):
         dh[pl.ds(C * c, C), :] = ds_[c, pl.ds(0, C), :]
         dl[pl.ds(C * c, C), :] = ds_[c, pl.ds(C, C), :]
     hi, lo = split(dy_far[...])
     dh[pl.ds(ROWS, ROWS), :] = hi
     dl[pl.ds(ROWS, ROWS), :] = lo
-    p_h.wait_recv()
+    kept["ph"].wait_recv()
     for ref, at in ((ht.at[pl.ds(half_h, 432)], 0), (ht_far, ROWS)):
         hi, lo = split(ref[...])
         hth[pl.ds(0, 432), pl.ds(at, ROWS)] = hi
         hth[pl.ds(432, 432), pl.ds(at, ROWS)] = lo
     gd_o[...] = dot3(hth[...], dh[...], dl[...], NN)
-    p_gu.wait_recv()
+    arrived([kept["pg", 0], kept["pg", 1]])
     for i, o in enumerate((gg_o, gu_o)):
         for c in range(2):
             hi, lo = split(far[c, i].reshape(C, HP))
@@ -341,18 +369,24 @@
             bl[i, pl.ds(ROWS + C * c, C), :] = lo
         o[...] = dot3(xth[...], bh[i], bl[i], NN)[:, :H]
 
-    for i, c, copies, o in ((0, 0, g00, out_o), (1, 0, g10, gtok_o), (0, 1, g01, out_o), (1, 1, g11, gtok_o)):
-        arrived(copies)
-        total = op[i, c, row8(h), :]
-        for k in range(7):
-            total = total + rg[i, c, k]
-        o[pl.ds(8 * c, 8), :] = total
+    for i, o in enumerate((out_o, gtok_o)):
+        arrived(kept["g", i, 0])
+        near = ring_sum(i, 0)
+        arrived(kept["g", i])
+        o[...] = near + rx[i]
     for c in sent:
         c.wait_send()
 
 
 def write(*refs):
-    copies = [pltpu.make_async_copy(refs[i], refs[5 + i], refs[10].at[i]) for i in range(5)]
+    copies = []
+    for i in range(5):
+        src, dst, sems = refs[i], refs[5 + i], refs[10]
+        n = PIECES[i]
+        rows = src.shape[0] // n
+        for k in range(n):
+            at = pl.ds(rows * k, rows)
+            copies.append(pltpu.make_async_copy(src.at[at], dst.at[at], sems.at[i, k]))
     for c in copies:
         c.start()
     for c in copies:
@@ -373,9 +407,9 @@
         v((2, 2, 2, 32, HP), F32),
         v((640, 256), BF16), v((864, 256), BF16),
         v((2, 256, HP), BF16), v((2, 256, HP), BF16), v((256, W), BF16), v((256, W), BF16),
-        v((2, 2, C, W), F32), v((2, 2, 7, 8, W), F32),
-        dma((4, 7)), dma((4, 7)), dma((2, 2, 8)), dma((2, 2, 8)), dma((2, 2, 8)), dma((2, 2, 8)),
-        dma((2, 2, 7)), dma((2, 2, 7)), dma((4,)), dma((4,)), dma((7,)),
+        v((2, 2, C, W), F32), v((2, 2, 3, 16, W), F32), v((2, 16, W), F32), v((2, 16, W), F32),
+        dma((2, 7)), dma((2, 7)), dma((2, 2, 8)), dma((2, 2, 8)), dma((2, 2, 8)), dma((2, 2, 8)),
+        dma((2, 2, 4)), dma((2, 2, 4)), dma((5,)), dma((5,)), dma((7,)),
     ]
     any_ = pl.BlockSpec(memory_space=pl.ANY)
     vmem = pl.BlockSpec(memory_space=pltpu.VMEM)
@@ -397,7 +431,7 @@
         out_shape=[jax.ShapeDtypeStruct(s, F32) for s in shapes],
         in_specs=[vmem] * 5,
         out_specs=[any_] * 5,
-        scratch_shapes=[dma((5,))],
+        scratch_shapes=[dma((5, max(PIECES)))],
     )(*results)
     return out, gtok, gg[None, None], gu[None, None], gd[None, None]
 

time: 54.4 us -> 50.3 us (0.925)
  the two profiles are of different devices: /device:TPU:0 before, /device:TPU:1 now
where the time goes in v4:
time: 50.3 us; the launch traced here: 50.2 us
  Pallas kernels  49.5 us (98%)
  between operations  0.64 us (1%)
    pallas_call x1, Pallas kernels, shards(): pl.pallas_call(kernel, out_shape=[v(s, F32) for s in shapes], in_specs=[h...  47.7 us
    pallas_call x1, Pallas kernels, shards(): pl.pallas_call(write, out_shape=[jax.ShapeDtypeStruct(s, F32) for s in sh...  1.82 us

profile of v4, /device:TPU:1, one launch (start us, length us, event | category | flops | bytes accessed | tf_op | source)
XLA Modules:
  0.0 50.2 jit_solution(1958933847204759633)
XLA Ops:
  0.6 47.7 %shard_map.92 = (f32[16,640]{1,0:T(8,128)S(1)}, f32[16,640]{1,0:T(8,128)S(1)}, f32[320,864]{1,0:T(8,128)S(1)}, f32[320,864]{1,0:T(8,128)S(1)}, f32[432,640]{1,0:T(8,128)S(1)}) custom-call(f32[16,640]{1,0:T(8,128)} %tok_in.1, f32[16,640]{1,0:T(8,128)} %cot_in.1, f32[864,640]{1,0:T(8,128)} %bitcast.5, f32[864,640]{1,0:T(8,128)} %bitcast.6, f32[864,640]{1,0:T(8,128)} %wd_in.1), custom_call_target="tpu_custom_call" | custom-call | tf_op jit(solution)/shard_map/pallas_call | solution.py:418
  48.4 1.8 %shard_map.93 = (f32[16,640]{1,0:T(8,128)}, f32[16,640]{1,0:T(8,128)}, f32[320,864]{1,0:T(8,128)}, f32[320,864]{1,0:T(8,128)}, f32[432,640]{1,0:T(8,128)}) custom-call(f32[16,640]{1,0:T(8,128)S(1)} %get-tuple-element.15.refs_0_, f32[16,640]{1,0:T(8,128)S(1)} %get-tuple-element.16.refs_1_, f32[320,864]{1,0:T(8,128)S(1)} %get-tuple-element.17.refs_2_, ...), custom_call_target="tpu_custom_call" | custom-call | tf_op jit(solution)/shard_map/pallas_call | solution.py:429

commit v5 on v4

--- a/solution.py
+++ b/solution.py
@@ -11,7 +11,6 @@
 F32 = jnp.float32
 BF16 = jnp.bfloat16
 NN = (((1,), (0,)), ((), ()))
-NT = (((1,), (1,)), ((), ()))
 ROWS = 128
 W = 640
 H = 864
@@ -21,10 +20,15 @@
 EX = 384
 SX, SY = pl.ds(0, CX), pl.ds(CX, HP - CX)
 GX, GY = pl.ds(0, EX), pl.ds(EX, HP - EX)
-GROUPS = ((0, 2), (2, 1))
+GROUPS = ((0, 1), (1, 1), (2, 1))
+COLUMNS = (pl.ds(0, 640),)
+FAR_DIRECT = True
 GROUPS_BACK = ((0, 1), (1, 2))
 PIECES = (1, 1, 1, 1, 1)
-ORDER = ("fx", "gu0", "fd", "bk0", "gu1", "bk1", "s00", "s01", "s10", "s11", "act0", "dy", "der0", "act1", "der1", "f00", "f10", "f11", "f01", "pr0", "xt", "pr1", "pb1", "r01", "pb0", "r11", "ht")
+ORDER = (
+    "fx", "gu0", "fd", "bk0", "gu1", "bk1", "s00", "s01", "s02", "s10", "s11", "s12", "act0", "dy", "der0",
+    "act1", "der1", "f00", "xt", "f10", "f11", "f01", "pr0", "pr1", "tt", "ht", "pb1", "gd", "pb0", "r01", "gw",
+)
 
 
 def split(v):
@@ -46,10 +50,11 @@
     tok_in, cot_in, wg_in, wu_in, wd_in,
     out_o, gtok_o, gg_o, gu_o, gd_o,
     xf, df, xs, ds_, wgf, wuf, wdf, wgh, wgl, wuh, wul, wdh, wdl,
+    wgth, wgtl, wuth, wutl, wdth, wdtl,
     part, r1, r2, r3, r4, s1, s3, full,
     xt, xt_far, dy_far, ht, ht_far, far,
     xth, hth, bh, bl, dh, dl,
-    op, rz, sz, rx,
+    op, rz, sz, rx, rf,
     a_s, a_r, c_s, c_r, e_s, e_r, g_s, g_r, p_s, p_r, l_s,
 ):
     rep = lax.axis_index("rep")
@@ -66,7 +71,10 @@
     def zdev(k):
         return (rep, w, ((z + k) % 4) * 2 + xh)
 
-    hdev = (rep, w, z * 2 + (1 - xh))
+    def odev(k):
+        return (rep, w, ((z + k) % 4) * 2 + (1 - xh))
+
+    hdev = odev(0)
     pdev = (1 - rep, w, h)
     sent = []
 
@@ -96,9 +104,11 @@
 
     lx = local(tok_in, xf.at[ring(0)], 0)
     ly = local(cot_in, df.at[ring(0)], 1)
-    lg = local(wg_in, wgf, 4)
-    lu = local(wu_in, wuf, 5)
-    ld = local(wd_in, wdf, 6)
+    lg = local(wg_in, wgf.at[pl.ds(0, H)], 2)
+    lu = local(wu_in, wuf.at[pl.ds(0, H)], 3)
+    ld = local(wd_in, wdf.at[pl.ds(0, H)], 4)
+    for ref in (wgf, wuf, wdf):
+        ref[pl.ds(H, HP - H), :] = jnp.zeros((HP - H, W), F32)
 
     barrier = pltpu.get_barrier_semaphore()
     peers = [ydev(k) for k in (2, 1, 3)] + [xdev] + [zdev(k) for k in (2, 1, 3)] + [hdev] + [pdev]
@@ -119,17 +129,15 @@
     ax = spread(tok_in, xf, 0)
     ad = spread(cot_in, df, 1)
 
-    def halves(src, hi_ref, lo_ref):
-        step = 32
-
+    def halves(src, hi_ref, lo_ref, turned_hi, turned_lo):
         def body(i, _):
-            at = pl.multiple_of(i * step, step)
-            hi, lo = split(src[pl.ds(at, step), :])
-            hi_ref[pl.ds(at, step), :] = hi
-            lo_ref[pl.ds(at, step), :] = lo
+            at = pl.ds(pl.multiple_of(i * 128, 128), 128)
+            v = src[at, :]
+            hi_ref[at, :], lo_ref[at, :] = split(v)
+            turned_hi[:, at], turned_lo[:, at] = split(v.T)
             return 0
 
-        lax.fori_loop(0, H // step, body, 0)
+        lax.fori_loop(0, HP // 128, body, 0)
 
     def stacked(src, dst, c):
         hi, lo = split(src[pl.ds(C * c, C), :])
@@ -227,57 +235,73 @@
     def whole(c, a):
         return full[c, a].reshape(C, HP)
 
-    def reduce_rows(i, c):
+    def reduce_rows(i, c, cols, part_no):
         return [
-            send(op.at[i, c, ring(0, k)], rz.at[i, c, k - 1], g_s.at[i, c, k], g_r.at[i, c, k], zdev(k))
+            send(
+                op.at[i, c, ring(0, k), cols], rz.at[i, c, k - 1, :, cols],
+                g_s.at[i, c, part_no, k], g_r.at[i, c, part_no, k], zdev(k),
+            )
             for k in (2, 1, 3)
         ]
 
     def ring_sum(i, c):
         return op[i, c, ring(0), :] + rz[i, c, 0] + rz[i, c, 1] + rz[i, c, 2]
+
+    def reduce_far(i, cols, part_no):
+        return [
+            send(
+                op.at[i, 1, ring(0, k), cols], rf.at[k, :, cols],
+                g_s.at[i, 1, part_no, k], g_r.at[i, 1, part_no, k], odev(k),
+            )
+            for k in (2, 1, 3, 0)
+        ]
 
     def reduce_on(i, first):
         arrived(first)
         sz[i] = ring_sum(i, 1)
-        return [send(sz.at[i], rx.at[i], g_s.at[i, 0, 0], g_r.at[i, 0, 0], hdev)]
+        return [send(sz.at[i], rx.at[i], g_s.at[i, 0, 0, 0], g_r.at[i, 0, 0, 0], hdev)]
 
     def project(c):
         hi, lo = split(whole(c, 0))
         op[0, c] = dot3(jnp.concatenate([hi, lo], axis=0), wdh[...], wdl[...], NN)
-        return reduce_rows(0, c)
+        return reduce_rows(0, c, pl.ds(0, W), 0)
 
     def pull_back(c):
-        acc = None
-        for i, (wh, wl) in enumerate(((wgh, wgl), (wuh, wul))):
+        terms = []
+        for i in range(2):
+            at = pl.ds(C * c, C)
             hi, lo = split(whole(c, 1 + i))
-            bh[i, pl.ds(C * c, C), :] = hi
-            bl[i, pl.ds(C * c, C), :] = lo
-            term = dot3(jnp.concatenate([hi, lo], axis=0), wh[...], wl[...], NN)
-            acc = term if acc is None else acc + term
-        op[1, c] = acc
-        return reduce_rows(1, c)
+            bh[i, at, :], bl[i, at, :] = hi, lo
+            terms.append(jnp.concatenate([hi, lo], axis=0))
+        copies = []
+        for part_no, cols in enumerate(COLUMNS):
+            op[1, c, :, cols] = dot3(terms[0], wgh[:, cols], wgl[:, cols], NN) + dot3(terms[1], wuh[:, cols], wul[:, cols], NN)
+            if c == 1 and FAR_DIRECT:
+                copies += reduce_far(1, cols, part_no)
+            else:
+                copies += reduce_rows(1, c, cols, part_no)
+        return copies
 
     def gate_up(c):
         arrived(kept.pop(("x", c)))
         stacked(xf, xs, c)
-        part[c, 0] = halved(dot3(xs[c], wgh[...], wgl[...], NT))
-        part[c, 1] = halved(dot3(xs[c], wuh[...], wul[...], NT))
-        return scatter(c, 0)
+        part[c, 0] = halved(dot3(xs[c], wgth[...], wgtl[...], NN))
+        gate = scatter(c, 0)
+        part[c, 1] = halved(dot3(xs[c], wuth[...], wutl[...], NN))
+        return gate, scatter(c, 1)
 
     def back_part(c):
         arrived(kept.pop(("d", c)))
         stacked(df, ds_, c)
-        part[c, 2] = halved(dot3(ds_[c], wdh[...], wdl[...], NT))
-        return scatter(c, 1)
-
-    for ref in (wgh, wgl, wuh, wul, wdh, wdl):
-        ref[pl.ds(H, HP - H), :] = jnp.zeros((HP - H, W), BF16)
+        part[c, 2] = halved(dot3(ds_[c], wdth[...], wdtl[...], NN))
+        return scatter(c, 2)
+
     lg.wait()
-    halves(wgf, wgh, wgl)
+    halves(wgf, wgh, wgl, wgth, wgtl)
     lu.wait()
-    halves(wuf, wuh, wul)
+    halves(wuf, wuh, wul, wuth, wutl)
     ld.wait()
-    halves(wdf, wdh, wdl)
+    halves(wdf, wdh, wdl, wdth, wdtl)
     lx.wait()
     ly.wait()
     kept = {("x", 0): ax[:3], ("d", 0): ad[:3]}
@@ -290,14 +314,17 @@
     half_h = pl.multiple_of(432 * rep, 16)
     far_h = pl.multiple_of(432 * (1 - rep), 16)
 
+    def do_gate_up(c):
+        kept["c", c, 0], kept["c", c, 1] = gate_up(c)
+
     def do_activate(c):
-        arrived(kept.pop(("d", c, 0)))
+        arrived(kept.pop(("d", c, 0)) + kept.pop(("d", c, 1)))
         copies, saved = activate(c)
         keep(("e", c, 0), copies)
         keep(("saved", c), saved)
 
     def do_derive(c):
-        arrived(kept.pop(("d", c, 1)))
+        arrived(kept.pop(("d", c, 2)))
         keep(("e", c, 1), derive(c, kept.pop(("saved", c))))
 
     def do_project(c):
@@ -331,49 +358,59 @@
         "r11": lambda: keep(("g", 1), reduce_on(1, kept.pop(("g", 1, 1)))),
     }
     for c in range(2):
-        steps[f"gu{c}"] = lambda c=c: keep(("c", c, 0), gate_up(c))
-        steps[f"bk{c}"] = lambda c=c: keep(("c", c, 1), back_part(c))
+        steps[f"gu{c}"] = lambda c=c: do_gate_up(c)
+        steps[f"bk{c}"] = lambda c=c: keep(("c", c, 2), back_part(c))
         steps[f"act{c}"] = lambda c=c: do_activate(c)
         steps[f"der{c}"] = lambda c=c: do_derive(c)
         steps[f"pr{c}"] = lambda c=c: do_project(c)
         steps[f"pb{c}"] = lambda c=c: do_pull_back(c)
+        for g in range(3):
+            steps[f"s{c}{g}"] = lambda c=c, g=g: keep(("d", c, g), scatter_on(c, g, kept.pop(("c", c, g))))
         for g in range(2):
-            steps[f"s{c}{g}"] = lambda c=c, g=g: keep(("d", c, g), scatter_on(c, g, kept.pop(("c", c, g))))
             steps[f"f{c}{g}"] = lambda c=c, g=g: keep(("f", c, g), gather_on(c, g, kept.pop(("e", c, g))))
+    def token_terms():
+        arrived([kept["px"], kept["py"]])
+        for ref, at in ((xt.at[pl.ds(half_x, 320)], 0), (xt_far, ROWS)):
+            hi, lo = split(ref[...])
+            xth[pl.ds(0, 320), pl.ds(at, ROWS)] = hi
+            xth[pl.ds(320, 320), pl.ds(at, ROWS)] = lo
+        for c in range(2):
+            dh[pl.ds(C * c, C), :] = ds_[c, pl.ds(0, C), :]
+            dl[pl.ds(C * c, C), :] = ds_[c, pl.ds(C, C), :]
+        dh[pl.ds(ROWS, ROWS), :], dl[pl.ds(ROWS, ROWS), :] = split(dy_far[...])
+
+    def down_gradient():
+        arrived([kept["ph"]])
+        for ref, at in ((ht.at[pl.ds(half_h, 432)], 0), (ht_far, ROWS)):
+            hi, lo = split(ref[...])
+            hth[pl.ds(0, 432), pl.ds(at, ROWS)] = hi
+            hth[pl.ds(432, 432), pl.ds(at, ROWS)] = lo
+        gd_o[...] = dot3(hth[...], dh[...], dl[...], NN)
+
+    def gate_up_gradients():
+        arrived([kept["pg", 0], kept["pg", 1]])
+        for i, o in enumerate((gg_o, gu_o)):
+            for c in range(2):
+                at = pl.ds(ROWS + C * c, C)
+                bh[i, at, :], bl[i, at, :] = split(far[c, i].reshape(C, HP))
+            o[...] = dot3(xth[...], bh[i], bl[i], NN)[:, :H]
+
+    steps["tt"] = token_terms
+    steps["gd"] = down_gradient
+    steps["gw"] = gate_up_gradients
     for name in ORDER:
         steps[name]()
 
-    kept["px"].wait_recv()
-    for ref, at in ((xt.at[pl.ds(half_x, 320)], 0), (xt_far, ROWS)):
-        hi, lo = split(ref[...])
-        xth[pl.ds(0, 320), pl.ds(at, ROWS)] = hi
-        xth[pl.ds(320, 320), pl.ds(at, ROWS)] = lo
-    kept["py"].wait_recv()
-    for c in range(2):
-        dh[pl.ds(C * c, C), :] = ds_[c, pl.ds(0, C), :]
-        dl[pl.ds(C * c, C), :] = ds_[c, pl.ds(C, C), :]
-    hi, lo = split(dy_far[...])
-    dh[pl.ds(ROWS, ROWS), :] = hi
-    dl[pl.ds(ROWS, ROWS), :] = lo
-    kept["ph"].wait_recv()
-    for ref, at in ((ht.at[pl.ds(half_h, 432)], 0), (ht_far, ROWS)):
-        hi, lo = split(ref[...])
-        hth[pl.ds(0, 432), pl.ds(at, ROWS)] = hi
-        hth[pl.ds(432, 432), pl.ds(at, ROWS)] = lo
-    gd_o[...] = dot3(hth[...], dh[...], dl[...], NN)
-    arrived([kept["pg", 0], kept["pg", 1]])
-    for i, o in enumerate((gg_o, gu_o)):
-        for c in range(2):
-            hi, lo = split(far[c, i].reshape(C, HP))
-            bh[i, pl.ds(ROWS + C * c, C), :] = hi
-            bl[i, pl.ds(ROWS + C * c, C), :] = lo
-        o[...] = dot3(xth[...], bh[i], bl[i], NN)[:, :H]
-
-    for i, o in enumerate((out_o, gtok_o)):
-        arrived(kept["g", i, 0])
-        near = ring_sum(i, 0)
-        arrived(kept["g", i])
-        o[...] = near + rx[i]
+    arrived(kept["g", 0, 0] + kept["g", 0])
+    out_o[...] = ring_sum(0, 0) + rx[0]
+    arrived(kept["g", 1, 0])
+    near = ring_sum(1, 0)
+    if FAR_DIRECT:
+        arrived(kept["g", 1, 1])
+        gtok_o[...] = near + rf[0] + rf[1] + rf[2] + rf[3]
+    else:
+        arrived(kept["g", 1])
+        gtok_o[...] = near + rx[1]
     for c in sent:
         c.wait_send()
 
@@ -399,7 +436,7 @@
     cy = HP - CX
     scratch = [
         v((ROWS, W), F32), v((ROWS, W), F32), v((2, 2 * C, W), BF16), v((2, 2 * C, W), BF16),
-        *[v((H, W), F32)] * 3, *[v((HP, W), BF16)] * 6,
+        *[v((HP, W), F32)] * 3, *[v((HP, W), BF16)] * 6, *[v((W, HP), BF16)] * 6,
         v((2, 3, 2, 32, HP), F32), v((2, 3, 32, CX), F32), v((2, 3, 3, 8, CX), F32),
         v((2, 3, 3, 2, 8, cy), F32), v((2, 3, 8, cy), F32), v((2, 3, 32, CX), F32),
         v((2, 3, 2, 8, cy), F32), v((2, 3, 2, 32, HP), F32),
@@ -407,9 +444,9 @@
         v((2, 2, 2, 32, HP), F32),
         v((640, 256), BF16), v((864, 256), BF16),
         v((2, 256, HP), BF16), v((2, 256, HP), BF16), v((256, W), BF16), v((256, W), BF16),
-        v((2, 2, C, W), F32), v((2, 2, 3, 16, W), F32), v((2, 16, W), F32), v((2, 16, W), F32),
-        dma((2, 7)), dma((2, 7)), dma((2, 2, 8)), dma((2, 2, 8)), dma((2, 2, 8)), dma((2, 2, 8)),
-        dma((2, 2, 4)), dma((2, 2, 4)), dma((5,)), dma((5,)), dma((7,)),
+        v((2, 2, C, W), F32), v((2, 2, 3, 16, W), F32), v((2, 16, W), F32), v((2, 16, W), F32), v((4, 16, W), F32),
+        dma((2, 7)), dma((2, 7)), dma((2, 3, 8)), dma((2, 3, 8)), dma((2, 2, 8)), dma((2, 2, 8)),
+        dma((2, 2, 2, 4)), dma((2, 2, 2, 4)), dma((5,)), dma((5,)), dma((5,)),
     ]
     any_ = pl.BlockSpec(memory_space=pl.ANY)
     vmem = pl.BlockSpec(memory_space=pltpu.VMEM)

time: 50.3 us -> 48 us (0.954)
  the two profiles are of different devices: /device:TPU:1 before, /device:TPU:0 now
where the time goes in v5:
time: 48 us; the launch traced here: 47.6 us
  Pallas kernels  46.9 us (98%)
  between operations  0.64 us (1%)
    pallas_call x1, Pallas kernels, shards(): pl.pallas_call(kernel, out_shape=[v(s, F32) for s in shapes], in_specs=[h...  45.1 us
    pallas_call x1, Pallas kernels, shards(): pl.pallas_call(write, out_shape=[jax.ShapeDtypeStruct(s, F32) for s in sh...  1.82 us

profile of v5, /device:TPU:0, one launch (start us, length us, event | category | flops | bytes accessed | tf_op | source)
XLA Modules:
  0.0 47.6 jit_solution(13341647031756384821)
XLA Ops:
  0.6 45.1 %shard_map.92 = (f32[16,640]{1,0:T(8,128)S(1)}, f32[16,640]{1,0:T(8,128)S(1)}, f32[320,864]{1,0:T(8,128)S(1)}, f32[320,864]{1,0:T(8,128)S(1)}, f32[432,640]{1,0:T(8,128)S(1)}) custom-call(f32[16,640]{1,0:T(8,128)} %tok_in.1, f32[16,640]{1,0:T(8,128)} %cot_in.1, f32[864,640]{1,0:T(8,128)} %bitcast.5, f32[864,640]{1,0:T(8,128)} %bitcast.6, f32[864,640]{1,0:T(8,128)} %wd_in.1), custom_call_target="tpu_custom_call" | custom-call | tf_op jit(solution)/shard_map/pallas_call | solution.py:455
  45.7 1.8 %shard_map.93 = (f32[16,640]{1,0:T(8,128)}, f32[16,640]{1,0:T(8,128)}, f32[320,864]{1,0:T(8,128)}, f32[320,864]{1,0:T(8,128)}, f32[432,640]{1,0:T(8,128)}) custom-call(f32[16,640]{1,0:T(8,128)S(1)} %get-tuple-element.15.refs_0_, f32[16,640]{1,0:T(8,128)S(1)} %get-tuple-element.16.refs_1_, f32[320,864]{1,0:T(8,128)S(1)} %get-tuple-element.17.refs_2_, ...), custom_call_target="tpu_custom_call" | custom-call | tf_op jit(solution)/shard_map/pallas_call | solution.py:466

commit v6 on v5

--- a/solution.py
+++ b/solution.py
@@ -17,18 +17,16 @@
 HP = 896
 C = 64
 CX = 512
-EX = 384
+EX = (512, 384)
 SX, SY = pl.ds(0, CX), pl.ds(CX, HP - CX)
-GX, GY = pl.ds(0, EX), pl.ds(EX, HP - EX)
+GX = [pl.ds(0, e) for e in EX]
+GY = [pl.ds(e, HP - e) for e in EX]
 GROUPS = ((0, 1), (1, 1), (2, 1))
 COLUMNS = (pl.ds(0, 640),)
 FAR_DIRECT = True
 GROUPS_BACK = ((0, 1), (1, 2))
 PIECES = (1, 1, 1, 1, 1)
-ORDER = (
-    "fx", "gu0", "fd", "bk0", "gu1", "bk1", "s00", "s01", "s02", "s10", "s11", "s12", "act0", "dy", "der0",
-    "act1", "der1", "f00", "xt", "f10", "f11", "f01", "pr0", "pr1", "tt", "ht", "pb1", "gd", "pb0", "r01", "gw",
-)
+ORDER = ("fx", "gu0", "fd", "bk0", "gu1", "s00", "s01", "bk1", "s02", "s10", "s11", "s12", "act0", "dy", "der0", "act1", "der1", "f00", "xt", "f10", "f11", "f01", "pr0", "pr1", "tt", "ht", "pb1", "gd", "pb0", "r01", "gw")
 
 
 def split(v):
@@ -198,9 +196,9 @@
     def gather(c, g):
         lo, n = GROUPS_BACK[g]
         arrays = pl.ds(lo, n)
-        mine = full.at[c, arrays, xl, row8(y), GY]
+        mine = full.at[c, arrays, xl, row8(y), GY[g]]
         out = [send(mine, mine, e_s.at[c, g, 0], e_r.at[c, g, 0], xdev)]
-        mine = full.at[c, arrays, xl, row8(y), GX]
+        mine = full.at[c, arrays, xl, row8(y), GX[g]]
         for k in (2, 1, 3):
             out.append(send(mine, mine, e_s.at[c, g, k], e_r.at[c, g, k], ydev(k)))
         return out
@@ -210,11 +208,11 @@
         arrays = pl.ds(lo, n)
         out = []
         arrived(first[:1])
-        pair = full.at[c, arrays, :, row8(y), GY]
+        pair = full.at[c, arrays, :, row8(y), GY[g]]
         for k in (2, 1, 3):
             out.append(send(pair, pair, e_s.at[c, g, 3 + k], e_r.at[c, g, 3 + k], ydev(k)))
         arrived(first[1:])
-        half = full.at[c, arrays, xl, :, GX]
+        half = full.at[c, arrays, xl, :, GX[g]]
         out.append(send(half, half, e_s.at[c, g, 7], e_r.at[c, g, 7], xdev))
         return out
 
@@ -253,7 +251,7 @@
                 op.at[i, 1, ring(0, k), cols], rf.at[k, :, cols],
                 g_s.at[i, 1, part_no, k], g_r.at[i, 1, part_no, k], odev(k),
             )
-            for k in (2, 1, 3, 0)
+            for k in (0, 2, 1, 3)
         ]
 
     def reduce_on(i, first):

time: 48 us -> 47.5 us (0.990)
  no operation moved by 1% of the time
where the time goes in v6:
time: 47.5 us; the launch traced here: 47.4 us
  Pallas kernels  46.8 us (99%)
  between operations  0.64 us (1%)
    pallas_call x1, Pallas kernels, shards(): pl.pallas_call(kernel, out_shape=[v(s, F32) for s in shapes], in_specs=[h...  45 us
    pallas_call x1, Pallas kernels, shards(): pl.pallas_call(write, out_shape=[jax.ShapeDtypeStruct(s, F32) for s in sh...  1.82 us

profile of v6, /device:TPU:0, one launch (start us, length us, event | category | flops | bytes accessed | tf_op | source)
XLA Modules:
  0.0 47.4 jit_solution(12125395753491135685)
XLA Ops:
  0.6 45.0 %shard_map.92 = (f32[16,640]{1,0:T(8,128)S(1)}, f32[16,640]{1,0:T(8,128)S(1)}, f32[320,864]{1,0:T(8,128)S(1)}, f32[320,864]{1,0:T(8,128)S(1)}, f32[432,640]{1,0:T(8,128)S(1)}) custom-call(f32[16,640]{1,0:T(8,128)} %tok_in.1, f32[16,640]{1,0:T(8,128)} %cot_in.1, f32[864,640]{1,0:T(8,128)} %bitcast.5, f32[864,640]{1,0:T(8,128)} %bitcast.6, f32[864,640]{1,0:T(8,128)} %wd_in.1), custom_call_target="tpu_custom_call" | custom-call | tf_op jit(solution)/shard_map/pallas_call | solution.py:453
  45.6 1.8 %shard_map.93 = (f32[16,640]{1,0:T(8,128)}, f32[16,640]{1,0:T(8,128)}, f32[320,864]{1,0:T(8,128)}, f32[320,864]{1,0:T(8,128)}, f32[432,640]{1,0:T(8,128)}) custom-call(f32[16,640]{1,0:T(8,128)S(1)} %get-tuple-element.15.refs_0_, f32[16,640]{1,0:T(8,128)S(1)} %get-tuple-element.16.refs_1_, f32[320,864]{1,0:T(8,128)S(1)} %get-tuple-element.17.refs_2_, ...), custom_call_target="tpu_custom_call" | custom-call | tf_op jit(solution)/shard_map/pallas_call | solution.py:464

commit v7 on v6

--- a/solution.py
+++ b/solution.py
@@ -19,6 +19,8 @@
 CX = 512
 EX = (512, 384)
 SX, SY = pl.ds(0, CX), pl.ds(CX, HP - CX)
+LANES = (SX, SY)
+SIDES = (0, 1)
 GX = [pl.ds(0, e) for e in EX]
 GY = [pl.ds(e, HP - e) for e in EX]
 GROUPS = ((0, 1), (1, 1), (2, 1))
@@ -26,7 +28,10 @@
 FAR_DIRECT = True
 GROUPS_BACK = ((0, 1), (1, 2))
 PIECES = (1, 1, 1, 1, 1)
-ORDER = ("fx", "gu0", "fd", "bk0", "gu1", "s00", "s01", "bk1", "s02", "s10", "s11", "s12", "act0", "dy", "der0", "act1", "der1", "f00", "xt", "f10", "f11", "f01", "pr0", "pr1", "tt", "ht", "pb1", "gd", "pb0", "r01", "gw")
+ORDER = (
+    "fx", "gu0", "fd", "bk0", "gu1", "x00", "y00", "x01", "y01", "bk1", "x02", "y02", "x10", "x11", "x12", "y10", "y11", "y12",
+    "act0", "dy", "der0", "act1", "der1", "f00", "f10", "f11", "f01", "pr0", "xt", "pr1", "ht", "tt", "pb1", "gd", "pb0", "r01", "gw",
+)
 
 
 def split(v):
@@ -163,7 +168,7 @@
             )
         return out
 
-    def scatter_on(c, g, first):
+    def scatter_x(c, g, first):
         lo, n = GROUPS[g]
         arrays = pl.ds(lo, n)
         arrived(first[:1])
@@ -177,31 +182,34 @@
                     c_s.at[c, g, 3 + k], c_r.at[c, g, 3 + k], ydev(k),
                 )
             )
+        return out
+
+    def scatter_y(c, g, first):
+        lo, n = GROUPS[g]
+        arrays = pl.ds(lo, n)
         arrived(first[1:])
         for a in range(lo, lo + n):
             s3[c, a] = part[c, a, :, row8(y), SY] + r3[c, 0, a] + r3[c, 1, a] + r3[c, 2, a]
-        out.append(
+        return [
             send(
                 s3.at[c, arrays, 1 - xl], r4.at[c, arrays],
                 c_s.at[c, g, 7], c_r.at[c, g, 7], xdev,
             )
-        )
-        return out
-
-    def summed(c, a):
-        left = s1[c, a, row8(y), :] + r2[c, 0, a] + r2[c, 1, a] + r2[c, 2, a]
-        right = s3[c, a, xl] + r4[c, a]
-        return jnp.concatenate([left, right], axis=1)
-
-    def gather(c, g):
+        ]
+
+    def summed(c, a, side):
+        if side == 0:
+            return s1[c, a, row8(y), :] + r2[c, 0, a] + r2[c, 1, a] + r2[c, 2, a]
+        return s3[c, a, xl] + r4[c, a]
+
+    def gather(c, g, side):
         lo, n = GROUPS_BACK[g]
         arrays = pl.ds(lo, n)
-        mine = full.at[c, arrays, xl, row8(y), GY[g]]
-        out = [send(mine, mine, e_s.at[c, g, 0], e_r.at[c, g, 0], xdev)]
+        if side == 1:
+            mine = full.at[c, arrays, xl, row8(y), GY[g]]
+            return [send(mine, mine, e_s.at[c, g, 0], e_r.at[c, g, 0], xdev)]
         mine = full.at[c, arrays, xl, row8(y), GX[g]]
-        for k in (2, 1, 3):
-            out.append(send(mine, mine, e_s.at[c, g, k], e_r.at[c, g, k], ydev(k)))
-        return out
+        return [send(mine, mine, e_s.at[c, g, k], e_r.at[c, g, k], ydev(k)) for k in (2, 1, 3)]
 
     def gather_on(c, g, first):
         lo, n = GROUPS_BACK[g]
@@ -216,19 +224,17 @@
         out.append(send(half, half, e_s.at[c, g, 7], e_r.at[c, g, 7], xdev))
         return out
 
-    def activate(c):
-        gate = summed(c, 0)
-        up = summed(c, 1)
+    def activate(c, side):
+        gate = summed(c, 0, side)
+        up = summed(c, 1, side)
         logistic = 1.0 / (1.0 + jnp.exp(-gate))
-        full[c, 0, xl, row8(y), :] = gate * logistic * up
-        return gather(c, 0), (gate, up, logistic)
-
-    def derive(c, saved):
-        gate, up, logistic = saved
-        back = summed(c, 2)
-        full[c, 1, xl, row8(y), :] = back * up * logistic * (1.0 + gate * (1.0 - logistic))
-        full[c, 2, xl, row8(y), :] = back * gate * logistic
-        return gather(c, 1)
+        full[c, 0, xl, row8(y), LANES[side]] = gate * logistic * up
+        return gate, up, logistic
+
+    def derive(c, side, gate, up, logistic):
+        back = summed(c, 2, side)
+        full[c, 1, xl, row8(y), LANES[side]] = back * up * logistic * (1.0 + gate * (1.0 - logistic))
+        full[c, 2, xl, row8(y), LANES[side]] = back * gate * logistic
 
     def whole(c, a):
         return full[c, a].reshape(C, HP)
@@ -315,15 +321,26 @@
     def do_gate_up(c):
         kept["c", c, 0], kept["c", c, 1] = gate_up(c)
 
+    def by_side(copies, side):
+        return copies[:3] if side == 0 else copies[3:]
+
     def do_activate(c):
-        arrived(kept.pop(("d", c, 0)) + kept.pop(("d", c, 1)))
-        copies, saved = activate(c)
-        keep(("e", c, 0), copies)
-        keep(("saved", c), saved)
+        copies = [None, None]
+        gate, up = kept.pop(("d", c, 0)), kept.pop(("d", c, 1))
+        for side in SIDES:
+            arrived(by_side(gate, side) + by_side(up, side))
+            keep(("saved", c, side), activate(c, side))
+            copies[side] = gather(c, 0, side)
+        keep(("e", c, 0), copies[1] + copies[0])
 
     def do_derive(c):
-        arrived(kept.pop(("d", c, 2)))
-        keep(("e", c, 1), derive(c, kept.pop(("saved", c))))
+        copies = [None, None]
+        back = kept.pop(("d", c, 2))
+        for side in (0, 1):
+            arrived(by_side(back, side))
+            derive(c, side, *kept.pop(("saved", c, side)))
+            copies[side] = gather(c, 1, side)
+        keep(("e", c, 1), copies[1] + copies[0])
 
     def do_project(c):
         arrived(kept.pop(("f", c, 0)))
@@ -363,7 +380,10 @@
         steps[f"pr{c}"] = lambda c=c: do_project(c)
         steps[f"pb{c}"] = lambda c=c: do_pull_back(c)
         for g in range(3):
-            steps[f"s{c}{g}"] = lambda c=c, g=g: keep(("d", c, g), scatter_on(c, g, kept.pop(("c", c, g))))
+            steps[f"x{c}{g}"] = lambda c=c, g=g: keep(("dx", c, g), scatter_x(c, g, kept["c", c, g]))
+            steps[f"y{c}{g}"] = lambda c=c, g=g: keep(
+                ("d", c, g), kept.pop(("dx", c, g)) + scatter_y(c, g, kept.pop(("c", c, g)))
+            )
         for g in range(2):
             steps[f"f{c}{g}"] = lambda c=c, g=g: keep(("f", c, g), gather_on(c, g, kept.pop(("e", c, g))))
     def token_terms():

time: 47.5 us -> 47.1 us (level)
  no operation moved by 1% of the time
where the time goes in v7:
time: 47.1 us; the launch traced here: 47 us
  Pallas kernels  46.4 us (99%)
  between operations  0.64 us (1%)
    pallas_call x1, Pallas kernels, shards(): pl.pallas_call(kernel, out_shape=[v(s, F32) for s in shapes], in_specs=[h...  44.6 us
    pallas_call x1, Pallas kernels, shards(): pl.pallas_call(write, out_shape=[jax.ShapeDtypeStruct(s, F32) for s in sh...  1.82 us

profile of v7, /device:TPU:0, one launch (start us, length us, event | category | flops | bytes accessed | tf_op | source)
XLA Modules:
  0.0 47.0 jit_solution(515480940058650229)
XLA Ops:
  0.6 44.6 %shard_map.92 = (f32[16,640]{1,0:T(8,128)S(1)}, f32[16,640]{1,0:T(8,128)S(1)}, f32[320,864]{1,0:T(8,128)S(1)}, f32[320,864]{1,0:T(8,128)S(1)}, f32[432,640]{1,0:T(8,128)S(1)}) custom-call(f32[16,640]{1,0:T(8,128)} %tok_in.1, f32[16,640]{1,0:T(8,128)} %cot_in.1, f32[864,640]{1,0:T(8,128)} %bitcast.5, f32[864,640]{1,0:T(8,128)} %bitcast.6, f32[864,640]{1,0:T(8,128)} %wd_in.1), custom_call_target="tpu_custom_call" | custom-call | tf_op jit(solution)/shard_map/pallas_call | solution.py:473
  45.2 1.8 %shard_map.93 = (f32[16,640]{1,0:T(8,128)}, f32[16,640]{1,0:T(8,128)}, f32[320,864]{1,0:T(8,128)}, f32[320,864]{1,0:T(8,128)}, f32[432,640]{1,0:T(8,128)}) custom-call(f32[16,640]{1,0:T(8,128)S(1)} %get-tuple-element.15.refs_0_, f32[16,640]{1,0:T(8,128)S(1)} %get-tuple-element.16.refs_1_, f32[320,864]{1,0:T(8,128)S(1)} %get-tuple-element.17.refs_2_, ...), custom_call_target="tpu_custom_call" | custom-call | tf_op jit(solution)/shard_map/pallas_call | solution.py:484

commit v8 on v7

--- a/solution.py
+++ b/solution.py
@@ -17,12 +17,12 @@
 HP = 896
 C = 64
 CX = 512
-EX = (512, 384)
+EX = ((512, 512), (512, 384))
 SX, SY = pl.ds(0, CX), pl.ds(CX, HP - CX)
 LANES = (SX, SY)
 SIDES = (0, 1)
-GX = [pl.ds(0, e) for e in EX]
-GY = [pl.ds(e, HP - e) for e in EX]
+GX = [[pl.ds(0, e) for e in row] for row in EX]
+GY = [[pl.ds(e, HP - e) for e in row] for row in EX]
 GROUPS = ((0, 1), (1, 1), (2, 1))
 COLUMNS = (pl.ds(0, 640),)
 FAR_DIRECT = True
@@ -206,9 +206,9 @@
         lo, n = GROUPS_BACK[g]
         arrays = pl.ds(lo, n)
         if side == 1:
-            mine = full.at[c, arrays, xl, row8(y), GY[g]]
+            mine = full.at[c, arrays, xl, row8(y), GY[c][g]]
             return [send(mine, mine, e_s.at[c, g, 0], e_r.at[c, g, 0], xdev)]
-        mine = full.at[c, arrays, xl, row8(y), GX[g]]
+        mine = full.at[c, arrays, xl, row8(y), GX[c][g]]
         return [send(mine, mine, e_s.at[c, g, k], e_r.at[c, g, k], ydev(k)) for k in (2, 1, 3)]
 
     def gather_on(c, g, first):
@@ -216,11 +216,11 @@
         arrays = pl.ds(lo, n)
         out = []
         arrived(first[:1])
-        pair = full.at[c, arrays, :, row8(y), GY[g]]
+        pair = full.at[c, arrays, :, row8(y), GY[c][g]]
         for k in (2, 1, 3):
             out.append(send(pair, pair, e_s.at[c, g, 3 + k], e_r.at[c, g, 3 + k], ydev(k)))
         arrived(first[1:])
-        half = full.at[c, arrays, xl, :, GX[g]]
+        half = full.at[c, arrays, xl, :, GX[c][g]]
         out.append(send(half, half, e_s.at[c, g, 7], e_r.at[c, g, 7], xdev))
         return out
 

time: 47.1 us -> 47.3 us (level)
  no operation moved by 1% of the time
where the time goes in v8:
time: 47.3 us; the launch traced here: 47.2 us
  Pallas kernels  46.5 us (98%)
  between operations  0.64 us (1%)
    pallas_call x1, Pallas kernels, shards(): pl.pallas_call(kernel, out_shape=[v(s, F32) for s in shapes], in_specs=[h...  44.7 us
    pallas_call x1, Pallas kernels, shards(): pl.pallas_call(write, out_shape=[jax.ShapeDtypeStruct(s, F32) for s in sh...  1.82 us

profile of v8, /device:TPU:0, one launch (start us, length us, event | category | flops | bytes accessed | tf_op | source)
XLA Modules:
  0.0 47.2 jit_solution(13884412727518228423)
XLA Ops:
  0.6 44.7 %shard_map.92 = (f32[16,640]{1,0:T(8,128)S(1)}, f32[16,640]{1,0:T(8,128)S(1)}, f32[320,864]{1,0:T(8,128)S(1)}, f32[320,864]{1,0:T(8,128)S(1)}, f32[432,640]{1,0:T(8,128)S(1)}) custom-call(f32[16,640]{1,0:T(8,128)} %tok_in.1, f32[16,640]{1,0:T(8,128)} %cot_in.1, f32[864,640]{1,0:T(8,128)} %bitcast.5, f32[864,640]{1,0:T(8,128)} %bitcast.6, f32[864,640]{1,0:T(8,128)} %wd_in.1), custom_call_target="tpu_custom_call" | custom-call | tf_op jit(solution)/shard_map/pallas_call | solution.py:473
  45.4 1.8 %shard_map.93 = (f32[16,640]{1,0:T(8,128)}, f32[16,640]{1,0:T(8,128)}, f32[320,864]{1,0:T(8,128)}, f32[320,864]{1,0:T(8,128)}, f32[432,640]{1,0:T(8,128)}) custom-call(f32[16,640]{1,0:T(8,128)S(1)} %get-tuple-element.15.refs_0_, f32[16,640]{1,0:T(8,128)S(1)} %get-tuple-element.16.refs_1_, f32[320,864]{1,0:T(8,128)S(1)} %get-tuple-element.17.refs_2_, ...), custom_call_target="tpu_custom_call" | custom-call | tf_op jit(solution)/shard_map/pallas_call | solution.py:484
